TPU v7x, 32 devices: a whole 2x2x4 slice. The times are simulated.
32 devices in a mesh: group: 2 (over x), wide: 16 (over z, y, core).
Axes of the slice: x: 2, y: 2, z: 4, core: 2. Of those that a mesh axis runs over, the one named last changes fastest.
Arguments:
- stream_index: int32 [2], P('group'), parts along dimension 0, may hold values from 0 to 16777215
- forcing: bfloat16 [32, 1536, 1536], P('group', 'wide'), parts along dimension 0, may hold values from -144 to 144
Outputs:
- pressure: bfloat16 [32, 1536, 1536], P('group', 'wide'), parts along dimension 0
There are 2 independent parts, one for each index of `group`. A program takes and returns all parts, laid end to end along the dimension named above; each array names one. Nothing has to cross between parts.
All inputs are finite; a program needn't handle non-finite values.
Results may differ from a plain program's by a relative error of at most 0.0045.
Values may be sent and summed in bfloat16 or wider, within the bound.
No kernel may reach another device: no remote copies, remote signals or barrier semaphores. Data moves between devices by JAX's collectives and lax.ppermute only.
A program may use at most 192 MiB of HBM per device.

v0:
```python
import functools
import math

import jax
import jax.numpy as jnp
from jax import lax
from jax.experimental import pallas as pl
from jax.experimental.pallas import tpu as pltpu
from jax.sharding import PartitionSpec as P

LEN_X = 1536
LEN_Y = 1536
ITERS = 4


def with_halo(block, sides, width):
    for axis, dim in sides:
        count = lax.axis_size(axis)
        forward = [(i, i + 1) for i in range(count - 1)]
        backward = [(target, source) for source, target in forward]
        low = lax.ppermute(
            lax.slice_in_dim(block, block.shape[dim] - width, None, axis=dim), axis, forward
        )
        high = lax.ppermute(lax.slice_in_dim(block, 0, width, axis=dim), axis, backward)
        block = jnp.concatenate([low, block, high], axis=dim)
    return block


def scramble(value):
    value = value ^ value >> 16 & 65535
    value = value * 73244475
    value = value ^ value >> 16 & 65535
    value = value * 73244475
    value = value ^ value >> 16 & 65535
    return value


def cosine_basis(length):
    row_idx = lax.broadcasted_iota(jnp.int32, (length, length), 0)
    mode_idx = lax.broadcasted_iota(jnp.int32, (length, length), 1)
    phase = (2 * row_idx + 1) * mode_idx % (4 * length)
    angle = phase.astype(jnp.float32) * (math.pi / (2.0 * length))
    weights = jnp.where(mode_idx == 0, math.sqrt(1.0 / length), math.sqrt(2.0 / length))
    return (weights * jnp.cos(angle)).astype(jnp.bfloat16)


def coefficient_plane(stream_key, mode_z, depth):
    mode_x = lax.broadcasted_iota(jnp.int32, (LEN_X, LEN_Y), 0)
    mode_y = lax.broadcasted_iota(jnp.int32, (LEN_X, LEN_Y), 1)
    counter = (mode_z * LEN_X + mode_x) * LEN_Y + mode_y
    bits_a = scramble(2 * counter ^ stream_key)
    bits_b = scramble(2 * counter + 1 ^ stream_key)
    uniform_a = (bits_a >> 8 & 16777215).astype(jnp.float32) * 2.0 ** (-24) + 2.0 ** (-25)
    uniform_b = (bits_b >> 8 & 16777215).astype(jnp.float32) * 2.0 ** (-24) + 2.0 ** (-25)
    noise = jnp.sqrt(-2.0 * jnp.log(uniform_a)) * jnp.cos(2.0 * math.pi * uniform_b)
    freq_x = mode_x.astype(jnp.float32) * (math.pi / LEN_X)
    freq_y = mode_y.astype(jnp.float32) * (math.pi / LEN_Y)
    freq_z = mode_z.astype(jnp.float32) * (math.pi / depth)
    amplitude = 1.0 / jnp.sqrt(0.05 + freq_x * freq_x + freq_y * freq_y + freq_z * freq_z)
    return (amplitude * noise).astype(jnp.bfloat16)


def contract_last(left, table):
    return lax.dot_general(
        left, table, (((left.ndim - 1,), (1,)), ((), ())), preferred_element_type=jnp.float32
    )


def operate(wide_p, wide_k):
    center_p = wide_p[:, 1:-1]
    center_k = wide_k[:, 1:-1]
    total = 0.5 * (center_k + wide_k[:, 2:]) * (center_p - wide_p[:, 2:])
    total = total + 0.5 * (center_k + wide_k[:, :-2]) * (center_p - wide_p[:, :-2])
    for axis in (0, 2):
        widths = [(0, 0), (0, 0), (0, 0)]
        widths[axis] = (1, 1)
        padded_p = jnp.pad(center_p, widths)
        padded_k = jnp.pad(center_k, widths)
        size_here = center_p.shape[axis]
        for start in (0, 2):
            near_p = lax.slice_in_dim(padded_p, start, start + size_here, axis=axis)
            near_k = lax.slice_in_dim(padded_k, start, start + size_here, axis=axis)
            total = total + 0.5 * (center_k + near_k) * (center_p - near_p)
    return total


def plain_body(stream_index, forcing):
    depth = forcing.shape[0]
    planes_here = depth // lax.axis_size("wide")
    stream_key = scramble(stream_index[0] ^ 1540483477)
    basis_x = cosine_basis(LEN_X)
    basis_y = cosine_basis(LEN_Y)
    basis_z = cosine_basis(depth)
    first_mode = lax.axis_index("wide") * planes_here
    own_modes = first_mode + jnp.arange(planes_here, dtype=jnp.int32)

    def rows_for(mode_z):
        coeff = coefficient_plane(stream_key, mode_z, depth)
        return jnp.dot(basis_x, coeff, preferred_element_type=jnp.float32).astype(jnp.bfloat16)

    def both_axes(mode_z):
        return contract_last(rows_for(mode_z), basis_y).astype(jnp.bfloat16)

    planes = lax.map(both_axes, own_modes)
    block = lax.all_to_all(planes, "wide", split_axis=1, concat_axis=0, tiled=True)
    count_z, count_x, count_y = block.shape
    field = jnp.dot(
        basis_z, block.reshape(count_z, count_x * count_y), preferred_element_type=jnp.float32
    )
    field = field.reshape(count_z, count_x, count_y)
    perm = jnp.exp(1.5 * jnp.tanh(2.0 * field))
    source = forcing.astype(jnp.float32)
    theta = 27.9
    delta = 26.1
    sigma = theta / delta
    rho = 1.0 / sigma
    step = source / theta
    press = step
    perm_wide = with_halo(perm.astype(jnp.bfloat16), (("wide", 1),), 1).astype(perm.dtype)
    for count in range(ITERS - 1):
        press_wide = with_halo(press, (("wide", 1),), 1)
        resid = source - operate(press_wide, perm_wide)
        rho_next = 1.0 / (2.0 * sigma - rho)
        step = rho_next * rho * step + 2.0 * rho_next / delta * resid
        press = press + step
        rho = rho_next
    return press.astype(jnp.bfloat16)


WIDE = 16
DEPTH = 16
HALO = ITERS - 1
PARTS = 4
UNROLL = 2
TILE = 16
FOLD = 16
VMEM_LIMIT = 60 << 20
THETA = 27.9
DELTA = 26.1
SIN_PI = (
    3.141592640144167, -5.16771008404795, 2.550077528430638, -0.5982912997813382, 0.077657661199004
)
MULT = 73244475


def cos_turns(turns, amplitude, negative=False):
    coeffs = [c * math.sqrt(2.0 * amplitude) for c in SIN_PI]
    square = turns * turns
    poly = coeffs[4] * square + coeffs[3]
    for c in coeffs[2::-1]:
        poly = poly * square + c
    sine = poly * turns
    return sine * sine - amplitude if negative else amplitude - sine * sine


def turns_of(phase, period):
    return (phase - jnp.floor(phase * (1.0 / period) + 0.5) * period) * (1.0 / period)


def srl(value, count):
    return lax.shift_right_logical(value, jnp.int32(count))


def angle_tables(cos_out, sin_out, of_row, length, weighted):
    period = 4.0 * length

    def part(i, carry):
        r = lax.broadcasted_iota(jnp.int32, (8, 128), 0) + i * 8
        factor = of_row(r).astype(jnp.float32)
        at = pl.ds(pl.multiple_of(i * 8, 8), 8)
        for j in range(length // 128):
            k = lax.broadcasted_iota(jnp.int32, (8, 128), 1).astype(jnp.float32) + 128.0 * j
            phase = factor * k
            cosine = cos_turns(turns_of(phase, period), 1.0)
            sine = cos_turns(turns_of(phase - length, period), 1.0)
            if weighted:
                weight = jnp.where(k == 0.0, math.sqrt(1.0 / length), math.sqrt(2.0 / length))
                cosine = cosine * weight
                sine = sine * weight
            cos_out[at, j * 128 : (j + 1) * 128] = cosine
            sin_out[at, j * 128 : (j + 1) * 128] = sine
        return carry

    lax.fori_loop(0, cos_out.shape[0] // 8, part, 0)


def basis_into(out_ref, small, big):
    rows = small[0].shape[0]
    length = out_ref.shape[1]
    angle_tables(*small, lambda r: 2 * r + 1, length, True)
    angle_tables(*big, lambda t: 2 * rows * t, length, False)

    def group(g, carry):
        group_at = pl.ds(pl.multiple_of(g * 8, 8), 8)
        for j in range(length // 128):
            cols = slice(j * 128, (j + 1) * 128)
            big_cos = big[0][group_at, cols]
            big_sin = big[1][group_at, cols]
            for t in range(8):
                at = pl.ds(pl.multiple_of((g * 8 + t) * rows, rows), rows)
                value = small[0][:, cols] * big_cos[t : t + 1] - small[1][:, cols] * big_sin[t : t + 1]
                out_ref[at, cols] = value.astype(jnp.bfloat16)
        return carry

    lax.fori_loop(0, big[0].shape[0] // 8, group, 0)


def folded_basis_into(out_ref, small, big, first_row, count, tiles):
    length = out_ref.shape[1]

    def block_row(r):
        return 2 * (first_row + r // FOLD * count - HALO + r % FOLD * tiles) + 1

    angle_tables(*small, block_row, length, True)
    angle_tables(*big, lambda i: 2 * i, length, False)

    def device(d, carry):
        at = pl.ds(pl.multiple_of(d * FOLD, FOLD), FOLD)
        for i in range(tiles):
            to = pl.ds(pl.multiple_of((d * tiles + i) * FOLD, FOLD), FOLD)
            for j in range(length // 128):
                cols = slice(j * 128, (j + 1) * 128)
                value = small[0][at, cols] * big[0][i : i + 1, cols] - small[1][at, cols] * big[1][i : i + 1, cols]
                out_ref[to, cols] = value.astype(jnp.bfloat16)
        return carry

    lax.fori_loop(0, small[0].shape[0] // FOLD, device, 0)


def coefficients_into(out_ref, key, mode_z, depth, rows):
    const = 2.0 * math.log(2.0)
    key_low = key & 1023
    key_high = key & ~1023

    def part(i, carry):
        r = lax.broadcasted_iota(jnp.int32, (rows, 128), 0) + i * rows
        at = pl.ds(pl.multiple_of(i * rows, rows), rows)
        freq_x = r.astype(jnp.float32) * (math.pi / LEN_X)
        freq_z = mode_z.astype(jnp.float32) * (math.pi / depth)
        row_part = (0.05 + freq_x * freq_x + freq_z * freq_z) * -const
        base = (r + mode_z * LEN_X) * (2 * LEN_Y)
        lane = lax.broadcasted_iota(jnp.int32, (1, 128), 1)
        for j in range(LEN_Y // 128):
            if j % 4 == 0:
                top = (base + j * 256) ^ key_high
                top = top ^ srl(top, 16)
                delta = jnp.where(((top ^ key_low) & 1) == 0, MULT, -MULT)
            freq_y = (lane + j * 128).astype(jnp.float32) * (math.pi / LEN_Y)
            denom = row_part + freq_y * freq_y * -const
            a = (top ^ (((lane + (j % 4) * 128) * 2) ^ key_low)) * MULT
            b = a + delta
            a = (a ^ srl(a, 16)) * MULT
            b = (b ^ srl(b, 16)) * MULT
            a = srl(a ^ srl(a, 16), 8)
            b = (b ^ srl(b, 16)) >> 8
            u = a.astype(jnp.float32) * 2.0 ** (-24) + 2.0 ** (-25)
            turns = b.astype(jnp.float32) * 2.0 ** (-24) + 2.0 ** (-25)
            bits = jnp.minimum(jnp.log2(u), -1e-30)
            size = bits * lax.rsqrt(bits * denom)
            value = size * cos_turns(turns, const, negative=True)
            out_ref[at, j * 128 : (j + 1) * 128] = value.astype(jnp.bfloat16)
        return carry

    lax.fori_loop(0, LEN_X // rows, part, 0)


def transform_into(out_refs, left_ref, coef_ref, rows_ref, basis_ref):
    for n in range(0, LEN_Y, 256):
        cols = slice(n, n + 256)
        rows_ref[:, cols] = jnp.dot(
            left_ref[...], coef_ref[:, cols], preferred_element_type=jnp.float32
        ).astype(jnp.bfloat16)
    size = rows_ref.shape[0] // len(out_refs)
    for n in range(0, LEN_Y, 256):
        cols = slice(n, n + 256)
        value = contract_last(rows_ref[...], basis_ref[cols, :])
        for m, out_ref in enumerate(out_refs):
            out_ref[:, cols] = value[m * size : (m + 1) * size].astype(jnp.bfloat16)


def first_planes_kernel(
    scalars, out_ref, basis_out, folded_out, basis, folded, coef, rows, small_cos, small_sin, big_cos, big_sin, sem,
    *, depth, count, tiles
):
    key, index = scalars[0], scalars[1]
    basis_into(basis, (small_cos.at[pl.ds(0, 64)], small_sin.at[pl.ds(0, 64)]), (big_cos, big_sin))
    folded_basis_into(
        folded,
        (small_cos, small_sin),
        (big_cos.at[pl.ds(0, 8)], big_sin.at[pl.ds(0, 8)]),
        (index >> 3) * (8 * count),
        count,
        tiles,
    )
    copies = [
        pltpu.make_async_copy(basis, basis_out, sem.at[0]),
        pltpu.make_async_copy(folded, folded_out, sem.at[1]),
    ]
    for copy in copies:
        copy.start()
    coefficients_into(coef, key, index & 7, depth, 64)
    transform_into([out_ref], folded, coef, rows, basis)
    for copy in copies:
        copy.wait()


def first_planes(scalars, depth, count, tiles):
    total = 8 * tiles * FOLD
    bits = jnp.bfloat16
    return pl.pallas_call(
        functools.partial(first_planes_kernel, depth=depth, count=count, tiles=tiles),
        in_specs=[pl.BlockSpec(memory_space=pltpu.SMEM)],
        out_specs=[pl.BlockSpec(memory_space=pltpu.VMEM)] + [pl.BlockSpec(memory_space=pl.ANY)] * 2,
        out_shape=[
            jax.ShapeDtypeStruct((total, LEN_Y), bits),
            jax.ShapeDtypeStruct((LEN_X, LEN_X), bits),
            jax.ShapeDtypeStruct((total, LEN_X), bits),
        ],
        scratch_shapes=[
            pltpu.VMEM((LEN_X, LEN_X), bits),
            pltpu.VMEM((total, LEN_X), bits),
            pltpu.VMEM((LEN_X, LEN_Y), bits),
            pltpu.VMEM((total, LEN_Y), bits),
            pltpu.VMEM((8 * FOLD, LEN_X), jnp.float32),
            pltpu.VMEM((8 * FOLD, LEN_X), jnp.float32),
            pltpu.VMEM((LEN_X // 64, LEN_X), jnp.float32),
            pltpu.VMEM((LEN_X // 64, LEN_X), jnp.float32),
            pltpu.SemaphoreType.DMA((2,)),
        ],
        compiler_params=pltpu.CompilerParams(vmem_limit_bytes=VMEM_LIMIT),
        cost_estimate=pl.CostEstimate(flops=25_000_000_000, transcendentals=0, bytes_accessed=8_000_000),
        name="first_planes",
    )(scalars)


def shared_mode(index, depth):
    color = (index >> 1 ^ index >> 2) & 1
    return depth // 2 + 4 * color + 2 * (index & 1)


def more_planes_kernel(scalars, basis_in, folded_in, *refs, depth, flips, offset):
    out_refs = refs[:PARTS]
    basis, left, coef, rows, sem = refs[PARTS:]
    size = out_refs[0].shape[0]
    key, index = scalars[0], scalars[1]
    mode = shared_mode(index, depth) + offset
    copies = [pltpu.make_async_copy(basis_in, basis, sem.at[PARTS])]
    for n, flip in enumerate(flips):
        source = folded_in.at[pl.ds(pl.multiple_of((index & 7 ^ flip) * size, size), size), :]
        copies.append(pltpu.make_async_copy(source, left.at[pl.ds(n * size, size), :], sem.at[n]))
    for copy in copies:
        copy.start()
    coefficients_into(coef, key, mode, depth, 64)
    for copy in copies:
        copy.wait()
    transform_into(out_refs, left, coef, rows, basis)


def more_planes(scalars, basis, folded, depth, size, flips, offset):
    anywhere = pl.BlockSpec(memory_space=pl.ANY)
    return pl.pallas_call(
        functools.partial(more_planes_kernel, depth=depth, flips=flips, offset=offset),
        in_specs=[pl.BlockSpec(memory_space=pltpu.SMEM), anywhere, anywhere],
        out_specs=[pl.BlockSpec(memory_space=pltpu.VMEM)] * PARTS,
        out_shape=[jax.ShapeDtypeStruct((size, LEN_Y), jnp.bfloat16)] * PARTS,
        scratch_shapes=[
            pltpu.VMEM((LEN_X, LEN_X), jnp.bfloat16),
            pltpu.VMEM((PARTS * size, LEN_X), jnp.bfloat16),
            pltpu.VMEM((LEN_X, LEN_Y), jnp.bfloat16),
            pltpu.VMEM((PARTS * size, LEN_Y), jnp.bfloat16),
            pltpu.SemaphoreType.DMA((PARTS + 1,)),
        ],
        compiler_params=pltpu.CompilerParams(vmem_limit_bytes=VMEM_LIMIT),
        cost_estimate=pl.CostEstimate(flops=20_000_000_000, transcendentals=0, bytes_accessed=8_000_000),
        name="more_planes",
    )(scalars, basis, folded)


def folded_row(index, tiles):
    return index % FOLD * tiles + index // FOLD


def fold_kernel(f_ref, low_ref, high_ref, out_ref, edge):
    _, count, _ = f_ref.shape
    padded = out_ref.shape[1]
    shape = (padded, count + TILE)
    row = folded_row(lax.broadcasted_iota(jnp.int32, shape, 0), padded // FOLD)
    source = jnp.where(row < HALO, row + count, jnp.where(row < HALO + count, row - HALO, row))
    spread = (lax.broadcasted_iota(jnp.int32, shape, 1) == source).astype(jnp.bfloat16)

    @pl.when(pl.program_id(0) == 0)
    def _():
        edge[...] = jnp.zeros(edge.shape, edge.dtype)

    for m in range(f_ref.shape[0]):
        edge[0:HALO, :] = low_ref[m]
        edge[HALO : 2 * HALO, :] = high_ref[m]
        rows = jnp.concatenate([f_ref[m], edge[...]], axis=0)
        for n in range(0, LEN_Y, 512):
            cols = slice(n, n + 512)
            out_ref[m, :, cols] = jnp.dot(spread, rows[:, cols], preferred_element_type=jnp.float32).astype(
                jnp.bfloat16
            )


def fold(forcing, low, high, padded):
    depth, count, _ = forcing.shape
    return pl.pallas_call(
        fold_kernel,
        grid=(depth // 2,),
        in_specs=[
            pl.BlockSpec((2, count, LEN_Y), lambda z: (z, 0, 0)),
            pl.BlockSpec((2, HALO, LEN_Y), lambda z: (z, 0, 0)),
            pl.BlockSpec((2, HALO, LEN_Y), lambda z: (z, 0, 0)),
        ],
        out_specs=pl.BlockSpec((2, padded, LEN_Y), lambda z: (z, 0, 0)),
        out_shape=jax.ShapeDtypeStruct((depth, padded, LEN_Y), jnp.bfloat16),
        scratch_shapes=[pltpu.VMEM((TILE, LEN_Y), jnp.bfloat16)],
        compiler_params=pltpu.CompilerParams(vmem_limit_bytes=VMEM_LIMIT),
        cost_estimate=pl.CostEstimate(flops=1_300_000_000, transcendentals=0, bytes_accessed=10_000_000),
        name="fold",
    )(forcing, low, high)


def chebyshev():
    sigma = THETA / DELTA
    rho = 1.0 / sigma
    pairs = []
    for _ in range(ITERS - 1):
        rho_next = 1.0 / (2.0 * sigma - rho)
        pairs.append((rho_next * rho, 2.0 * rho_next / DELTA))
        rho = rho_next
    return pairs


def solve_kernel(scalars, slot_modes, forcing, block, *refs):
    planes = refs[:-12]
    out_ref, k_ref, f_ref, p_two, p_three, b_two, b_three, natural, stage, turned, sems, sem_out = refs[-12:]
    modes = block.shape[0]
    depth, padded, _ = k_ref.shape
    count = out_ref.shape[1]
    tiles = padded // FOLD
    blocks = LEN_Y // 128
    index = scalars[1]

    def cols(j):
        return slice(j * 128, (j + 1) * 128)

    def copies(t, slot):
        at = pl.ds(t * FOLD, FOLD)
        found = [pltpu.make_async_copy(block.at[:, at, :], stage.at[slot, pl.ds(0, modes)], sems.at[slot, 0])]
        for n, plane in enumerate(planes):
            found.append(pltpu.make_async_copy(plane.at[at, :], stage.at[slot, modes + n], sems.at[slot, n + 1]))
        return found

    for copy in copies(0, 0):
        copy.start()
    forcing_copy = pltpu.make_async_copy(forcing, f_ref, sems.at[2, 0])

    size = depth * FOLD
    row = lax.broadcasted_iota(jnp.int32, (size, size), 0)
    col = lax.broadcasted_iota(jnp.int32, (size, size), 1)
    mode = jnp.broadcast_to(slot_modes[...], (size, size))
    phase = ((2 * (row // FOLD) + 1) * mode).astype(jnp.float32)
    weight = jnp.where(mode == 0, math.sqrt(1.0 / depth), math.sqrt(2.0 / depth))
    cosine = cos_turns(turns_of(phase, 4.0 * depth), 1.0)
    mixing = jnp.where(row % FOLD == col % FOLD, weight * cosine, 0.0).astype(jnp.bfloat16)

    def inside(start):
        row = folded_row(lax.broadcasted_iota(jnp.int32, (FOLD, 128), 0) + start, tiles)
        outside = ((row < HALO) & (index == 0)) | ((row >= HALO + count) & (index == WIDE - 1))
        return jnp.where(outside, 0.0, 1.0)

    for t in range(tiles):
        slot = t % 2
        if t + 1 < tiles:
            for copy in copies(t + 1, 1 - slot):
                copy.start()
        else:
            forcing_copy.start()
        for copy in copies(t, slot):
            copy.wait()
        keep = inside(t * FOLD)
        for n in range(0, LEN_Y, 512):
            field = jnp.dot(
                mixing,
                stage[slot, :, :, n : n + 512].reshape(size, 512),
                preferred_element_type=jnp.float32,
            ).reshape(depth, FOLD, 512)
            for j in range(n // 128, n // 128 + 4):
                part = field[:, :, j * 128 - n : j * 128 - n + 128]
                value = jnp.exp(1.5 * jnp.tanh(2.0 * part)) * keep[None]
                k_ref[:, t * FOLD : t * FOLD + FOLD, cols(j)] = value.astype(jnp.bfloat16)
    forcing_copy.wait()
    lane = lax.broadcasted_iota(jnp.int32, (FOLD, 128), 1)
    nothing = jnp.zeros((FOLD, 128), jnp.bfloat16)

    def sweep(src, store):
        def tile(i, below, above):
            at = pl.ds(pl.multiple_of(i * FOLD, FOLD), FOLD)
            factor = inside(i * FOLD)

            def level(z, top, flows_z):
                outs = []
                next_flows = []
                k_all = [k_ref[z, at, cols(j)] for j in range(blocks)]
                p_all = [src[z, at, cols(j)] for j in range(blocks)]
                turns = [pltpu.roll(p, 127, 1) for p in p_all] + [nothing]
                k_turns = [pltpu.roll(k, 127, 1) for k in k_all] + [nothing]
                before = None
                for j in range(blocks):
                    k, p = k_all[j], p_all[j]
                    k_right = jnp.where(lane == 127, k_turns[j + 1], k_turns[j])
                    flow_y = (k + k_right) * (p - jnp.where(lane == 127, turns[j + 1], turns[j]))
                    flow_turn = pltpu.roll(flow_y, 1, 1)
                    left = jnp.where(lane == 0, -k * p if before is None else before, flow_turn)
                    before = flow_turn
                    if top:
                        flow_z = k * p
                    else:
                        flow_z = (k + k_ref[z + 1, at, cols(j)]) * (p - src[z + 1, at, cols(j)])
                    flow_x = (k + above(k_ref, z, j)) * (p - above(src, z, j))
                    flow_w = (k + below(k_ref, z, j)) * (p - below(src, z, j))
                    outs.append((flow_x + flow_w) + ((flow_y - left) + (flow_z - flows_z[j])))
                    next_flows.append(flow_z)
                for j in range(blocks):
                    store(z, i, j, at, outs[j].astype(jnp.float32), factor)
                return next_flows

            def group(g, flows_z):
                for u in range(UNROLL):
                    flows_z = level(g * UNROLL + u, False, flows_z)
                return flows_z

            flows = [-k_ref[0, at, cols(j)] * src[0, at, cols(j)] for j in range(blocks)]
            groups = depth // UNROLL - 1
            flows = lax.fori_loop(0, groups, group, flows)
            for u in range(UNROLL):
                z = groups * UNROLL + u
                flows = level(z, z == depth - 1, flows)

        def plain(step):
            def load(ref, z, j, i):
                return ref[z, pl.ds(pl.multiple_of((i + step) * FOLD, FOLD), FOLD), cols(j)]

            return load

        def first(ref, z, j):
            return pltpu.roll(ref[z, padded - FOLD : padded, cols(j)], 1, 0)

        def last(ref, z, j):
            return pltpu.roll(ref[z, 0:FOLD, cols(j)], FOLD - 1, 0)

        def inner(i, carry):
            tile(
                i,
                lambda ref, z, j: plain(-1)(ref, z, j, i),
                lambda ref, z, j: plain(1)(ref, z, j, i),
            )
            return carry

        tile(0, first, lambda ref, z, j: plain(1)(ref, z, j, 0))
        lax.fori_loop(1, tiles - 1, inner, 0)
        tile(tiles - 1, lambda ref, z, j: plain(-1)(ref, z, j, tiles - 1), last)

    (a1, b1), (a2, b2), (a3, b3) = chebyshev()

    def store_one(z, i, j, at, out, factor):
        source = f_ref[z, at, cols(j)].astype(jnp.float32)
        value = ((1.0 + a1) / THETA + b1) * source - (0.5 * b1 / THETA * factor) * out
        p_two[z, at, cols(j)] = value
        b_two[z, at, cols(j)] = value.astype(jnp.bfloat16)

    def store_two(z, i, j, at, out, factor):
        source = f_ref[z, at, cols(j)].astype(jnp.float32)
        value = (1.0 + a2) * p_two[z, at, cols(j)] + (b2 - a2 / THETA) * source - (0.5 * b2 * factor) * out
        p_three[z, at, cols(j)] = value
        b_three[z, at, cols(j)] = value.astype(jnp.bfloat16)

    def store_three(z, i, j, at, out, factor):
        source = f_ref[z, at, cols(j)].astype(jnp.float32)
        old = (1.0 + a3) * p_three[z, at, cols(j)] - a3 * p_two[z, at, cols(j)]
        value = old + (b3 * source - 0.5 * b3 * out)
        for n in range(FOLD // 8):
            to = pl.ds(i + 8 - HALO + 8 * n * tiles, 8, stride=tiles)
            natural[z * blocks + j, to, :] = value[8 * n : 8 * n + 8]

    sweep(f_ref, store_one)
    sweep(b_two, store_two)
    sweep(b_three, store_three)

    def leave(z, slot):
        return pltpu.make_async_copy(turned.at[slot], out_ref.at[z], sem_out.at[slot])

    for z in range(depth):
        slot = z % 2
        if z > 1:
            leave(z - 2, slot).wait()
        for j in range(blocks):
            turned[slot, :, cols(j)] = natural[z * blocks + j, 8 : 8 + count, :].astype(jnp.bfloat16)
        leave(z, slot).start()
    for z in (depth - 2, depth - 1):
        leave(z, z % 2).wait()


def solve(scalars, slot_modes, forcing, block, planes, count):
    depth, padded, _ = forcing.shape
    anywhere = pl.BlockSpec(memory_space=pl.ANY)
    narrow = pltpu.VMEM((depth, padded, LEN_Y), jnp.bfloat16)
    whole = pltpu.VMEM((depth, padded, LEN_Y), jnp.float32)
    return pl.pallas_call(
        solve_kernel,
        in_specs=[pl.BlockSpec(memory_space=pltpu.SMEM), pl.BlockSpec(memory_space=pltpu.VMEM)]
        + [anywhere] * (2 + len(planes)),
        out_specs=anywhere,
        out_shape=jax.ShapeDtypeStruct((depth, count, LEN_Y), jnp.bfloat16),
        scratch_shapes=[
            narrow,
            narrow,
            whole,
            whole,
            narrow,
            narrow,
            pltpu.VMEM((depth * LEN_Y // 128, padded + 8, 128), jnp.float32),
            pltpu.VMEM((2, depth, FOLD, LEN_Y), jnp.bfloat16),
            pltpu.VMEM((2, count, LEN_Y), jnp.bfloat16),
            pltpu.SemaphoreType.DMA((3, 1 + len(planes))),
            pltpu.SemaphoreType.DMA((2,)),
        ],
        compiler_params=pltpu.CompilerParams(vmem_limit_bytes=VMEM_LIMIT),
        name="solve",
    )(scalars, slot_modes, forcing, block, *planes)


def body(stream_index, forcing):
    depth, count, _ = forcing.shape
    index = lax.axis_index("wide")
    scalars = jnp.stack([scramble(stream_index[0] ^ 1540483477), index]).astype(jnp.int32)
    tiles = -(-(count + 2 * HALO) // FOLD)
    padded = tiles * FOLD
    own, basis, folded = first_planes(scalars, depth, count, tiles)
    groups = [list(range(8)), list(range(8, 16))]
    block = lax.all_to_all(
        own.reshape(8, padded, LEN_Y), "wide", 0, 0, axis_index_groups=groups, tiled=True
    )

    def pairwise(offset, bit):
        flips = (0, 1, bit, bit ^ 1)
        out = more_planes(scalars, basis, folded, depth, padded, flips, offset)
        return [out[0]] + [
            lax.ppermute(piece, "wide", [(i, i ^ flip) for i in range(WIDE)])
            for piece, flip in zip(out[1:], flips[1:])
        ]

    planes = pairwise(0, 4) + pairwise(1, 2)
    slot = lax.broadcasted_iota(jnp.int32, (1, depth * FOLD), 1) // FOLD
    flip = jnp.where(slot < 12, (slot & 1) ^ (slot & 2) << 1, (slot & 1) ^ (slot & 2))
    slot_modes = jnp.where(slot < 8, slot, shared_mode(index ^ flip, depth) + (slot >= 12))
    forward = [(i, i + 1) for i in range(WIDE - 1)]
    backward = [(target, source) for source, target in forward]
    low = lax.ppermute(forcing[:, -HALO:], "wide", forward)
    high = lax.ppermute(forcing[:, :HALO], "wide", backward)
    return solve(scalars, slot_modes, fold(forcing, low, high, padded), block, planes, count)


def solution(mesh):
    special = mesh.shape["wide"] == WIDE
    return jax.shard_map(
        body if special else plain_body,
        mesh=mesh,
        in_specs=(P("group"), P("group", "wide", None)),
        out_specs=P("group", "wide", None),
        check_vma=False,
    )
```

profile of v0, /device:TPU:18, one launch (start us, length us, event | category | flops | bytes accessed | tf_op | source)
XLA Modules:
  0.0 171.5 jit_solution(12120443073104313048)
XLA Ops:
  0.7 0.6 pad_add_fusion.scalars
  1.3 31.3 %first_planes.1 = (bf16[896,1536]{1,0:T(8,128)(2,1)}, bf16[1536,1536]{1,0:T(8,128)(2,1)}, bf16[896,1536]{1,0:T(8,128)(2,1)}) custom-call(s32[2]{0:T(128)} %pad_add_fusion.scalars), custom_call_target="tpu_custom_call" | custom-call | flops 24999999488 | bytes 8000000 | tf_op jit(solution)/shard_map/first_planes/pallas_call | solution.py:310
  32.5 3.8 %all-to-all-start = ((bf16[8,112,1536]{2,1,0:T(8,128)(2,1)}), bf16[8,112,1536]{2,1,0:T(8,128)(2,1)S(1)}, u32[]{:S(2)}, u32[]{:S(2)}) async-start(bf16[8,112,1536]{2,1,0:T(8,128)(2,1)} %bitcast.4), calls=%async_computation | async-start | bytes 5505024 | tf_op jit(solution)/shard_map/all_to_all | solution.py:643
  36.4 20.5 %more_planes.3 = (bf16[112,1536]{1,0:T(8,128)(2,1)}, bf16[112,1536]{1,0:T(8,128)(2,1)}, bf16[112,1536]{1,0:T(8,128)(2,1)}, bf16[112,1536]{1,0:T(8,128)(2,1)}) custom-call(s32[2]{0:T(128)} %pad_add_fusion.scalars, bf16[1536,1536]{1,0:T(8,128)(2,1)} %get-tuple-element.17.basis_in, bf16[896,1536]{1,0:T(8,128)(2,1)} %get-tuple-element.18.folded_in), custom_call_target="tpu_custom_call" | custom-call | flops 20000000000 | bytes 8000000 | tf_op jit(solution)/shard_map/more_planes/pallas_call | solution.py:361
  56.9 0.6 collective-permute-start.5
  57.5 1.7 collective-permute-start.6
  59.2 1.9 %fusion.2 = (bf16[16,3,1536]{2,1,0:T(4,128)(2,1)S(1)}, bf16[16,3,1536]{2,1,0:T(4,128)(2,1)}) fusion(bf16[16,96,1536]{2,1,0:T(8,128)(2,1)} %f_ref.1), kind=kLoop, calls=%fused_computation.10 | loop fusion | bytes 589824 | tf_op jit(solution)/shard_map/slice | solution.py:662
  61.1 2.4 %collective-permute-start = (bf16[16,3,1536]{2,1,0:T(4,128)(2,1)}, bf16[16,3,1536]{2,1,0:T(4,128)(2,1)}, u32[]{:S(2)}, u32[]{:S(2)}) collective-permute-start(bf16[16,3,1536]{2,1,0:T(4,128)(2,1)} %get-tuple-element.28), channel_id=1, source_target_pairs={{0,1},{1,2},{2,3},{3,4},{4,5},{5,6},{6,7},{7,8},{8,9},{9,10},{10,1... | collective-permute-start | bytes 442376 | tf_op jit(solution)/shard_map/ppermute | solution.py:661
  63.5 4.3 %collective-permute-start.1 = (bf16[16,3,1536]{2,1,0:T(4,128)(2,1)S(1)}, bf16[16,3,1536]{2,1,0:T(4,128)(2,1)}, u32[]{:S(2)}, u32[]{:S(2)}) collective-permute-start(bf16[16,3,1536]{2,1,0:T(4,128)(2,1)S(1)} %get-tuple-element.27), channel_id=1, source_target_pairs={{1,0},{2,1},{3,2},{4,3},{5,4},{6,5},{7,6},{8,7},{9,8},{10,9},{11,1... | collective-permute-start | bytes 442376 | tf_op jit(solution)/shard_map/ppermute | solution.py:662
  67.8 20.5 %more_planes.2 = (bf16[112,1536]{1,0:T(8,128)(2,1)}, bf16[112,1536]{1,0:T(8,128)(2,1)}, bf16[112,1536]{1,0:T(8,128)(2,1)}, bf16[112,1536]{1,0:T(8,128)(2,1)}) custom-call(s32[2]{0:T(128)} %pad_add_fusion.scalars, bf16[1536,1536]{1,0:T(8,128)(2,1)} %get-tuple-element.17.basis_in, bf16[896,1536]{1,0:T(8,128)(2,1)} %get-tuple-element.18.folded_in), custom_call_target="tpu_custom_call" | custom-call | flops 20000000000 | bytes 8000000 | tf_op jit(solution)/shard_map/more_planes/pallas_call | solution.py:361
  88.3 0.0 collective-permute-done.low_ref
  88.3 0.1 collective-permute-start.2
  88.4 1.8 %collective-permute-start.3 = (bf16[112,1536]{1,0:T(8,128)(2,1)}, bf16[112,1536]{1,0:T(8,128)(2,1)}, u32[]{:S(2)}, u32[]{:S(2)}) collective-permute-start(bf16[112,1536]{1,0:T(8,128)(2,1)} %get-tuple-element.21), channel_id=1, source_target_pairs={{0,4},{1,5},{2,6},{3,7},{4,0},{5,1},{6,2},{7,3},{8,12},{9,13},{10,... | collective-permute-start | bytes 1032200 | tf_op jit(solution)/shard_map/ppermute | solution.py:651
  90.2 0.0 collective-permute-done.5.refs_5_
  90.2 0.1 collective-permute-start.4
  90.3 0.6 compare_select_fusion.slot_modes
  90.9 8.2 %fold.1.forcing = bf16[16,112,1536]{2,1,0:T(8,128)(2,1)} custom-call(bf16[16,96,1536]{2,1,0:T(8,128)(2,1)} %f_ref.1, bf16[16,3,1536]{2,1,0:T(4,128)(2,1)} %collective-permute-done.low_ref, bf16[16,3,1536]{2,1,0:T(4,128)(2,1)} %collective-permute-done.1.high_ref), custom_call_target="tpu_custom_call" | custom-call | flops 1300000000 | bytes 10000000 | tf_op jit(solution)/shard_map/fold/pallas_call | solution.py:408
  99.1 0.0 collective-permute-done.7.refs_7_
  99.2 0.5 collective-permute-done.3.refs_2_
  99.7 0.3 copy-done.3
  99.9 6.2 %collective-permute-done.4.refs_3_ = bf16[112,1536]{1,0:T(8,128)(2,1)} collective-permute-done((bf16[112,1536]{1,0:T(8,128)(2,1)}, bf16[112,1536]{1,0:T(8,128)(2,1)}, u32[]{:S(2)}, u32[]{:S(2)}) %collective-permute-start.4) | collective-permute-done | bytes 344096 | tf_op jit(solution)/shard_map/ppermute | solution.py:651
  106.1 0.0 all-to-all-done.block
  106.1 1.5 copy-done
  107.7 63.7 %solve.1 = bf16[16,96,1536]{2,1,0:T(8,128)(2,1)} custom-call(s32[2]{0:T(128)} %pad_add_fusion.scalars, s32[1,256]{1,0:T(1,128)} %compare_select_fusion.slot_modes, bf16[16,112,1536]{2,1,0:T(8,128)(2,1)} %fold.1.forcing, bf16[8,112,1536]{2,1,0:T(8,128)(2,1)} %copy-done, bf16[112,1536]{1,0:T(8,128)(2,1)} %get-tuple-element.19.refs_0_, ...), custom_call_target="tpu_custom_call" | custom-call | tf_op jit(solution)/shard_map/solve/pallas_call | solution.py:611
  (10 shorter events, 0.0 us)
Async XLA Ops:
  32.5 73.6 %all-to-all-start = ((bf16[8,112,1536]{2,1,0:T(8,128)(2,1)}), bf16[8,112,1536]{2,1,0:T(8,128)(2,1)S(1)}, u32[]{:S(2)}, u32[]{:S(2)}) async-start(bf16[8,112,1536]{2,1,0:T(8,128)(2,1)} %bitcast.4), calls=%async_computation | async-start | bytes 5505024 | tf_op jit(solution)/shard_map/all_to_all | solution.py:643
  56.9 33.3 %collective-permute-start.5 = (bf16[112,1536]{1,0:T(8,128)(2,1)}, bf16[112,1536]{1,0:T(8,128)(2,1)S(1)}, u32[]{:S(2)}, u32[]{:S(2)}) collective-permute-start(bf16[112,1536]{1,0:T(8,128)(2,1)} %get-tuple-element.24), channel_id=1, source_target_pairs={{0,1},{1,0},{2,3},{3,2},{4,5},{5,4},{6,7},{7,6},{8,9},{9,8},{10,11... | collective-permute-start | bytes 1032200 | tf_op jit(solution)/shard_map/ppermute | solution.py:651
  57.5 41.6 %collective-permute-start.6 = (bf16[112,1536]{1,0:T(8,128)(2,1)}, bf16[112,1536]{1,0:T(8,128)(2,1)S(1)}, u32[]{:S(2)}, u32[]{:S(2)}) collective-permute-start(bf16[112,1536]{1,0:T(8,128)(2,1)} %get-tuple-element.25), channel_id=1, source_target_pairs={{0,2},{1,3},{2,0},{3,1},{4,6},{5,7},{6,4},{7,5},{8,10},{9,11},{10,... | collective-permute-start | bytes 1032200 | tf_op jit(solution)/shard_map/ppermute | solution.py:651
  59.2 40.0 %collective-permute-start.7 = (bf16[112,1536]{1,0:T(8,128)(2,1)}, bf16[112,1536]{1,0:T(8,128)(2,1)S(1)}, u32[]{:S(2)}, u32[]{:S(2)}) collective-permute-start(bf16[112,1536]{1,0:T(8,128)(2,1)} %get-tuple-element.26), channel_id=1, source_target_pairs={{0,3},{1,2},{2,1},{3,0},{4,7},{5,6},{6,5},{7,4},{8,11},{9,10},{10,... | collective-permute-start | bytes 1032200 | tf_op jit(solution)/shard_map/ppermute | solution.py:651
  61.1 27.2 %collective-permute-start = (bf16[16,3,1536]{2,1,0:T(4,128)(2,1)}, bf16[16,3,1536]{2,1,0:T(4,128)(2,1)}, u32[]{:S(2)}, u32[]{:S(2)}) collective-permute-start(bf16[16,3,1536]{2,1,0:T(4,128)(2,1)} %get-tuple-element.28), channel_id=1, source_target_pairs={{0,1},{1,2},{2,3},{3,4},{4,5},{5,6},{6,7},{7,8},{8,9},{9,10},{10,1... | collective-permute-start | bytes 442376 | tf_op jit(solution)/shard_map/ppermute | solution.py:661
  63.5 24.9 %collective-permute-start.1 = (bf16[16,3,1536]{2,1,0:T(4,128)(2,1)S(1)}, bf16[16,3,1536]{2,1,0:T(4,128)(2,1)}, u32[]{:S(2)}, u32[]{:S(2)}) collective-permute-start(bf16[16,3,1536]{2,1,0:T(4,128)(2,1)S(1)} %get-tuple-element.27), channel_id=1, source_target_pairs={{1,0},{2,1},{3,2},{4,3},{5,4},{6,5},{7,6},{8,7},{9,8},{10,9},{11,1... | collective-permute-start | bytes 442376 | tf_op jit(solution)/shard_map/ppermute | solution.py:662
  88.3 10.8 %collective-permute-start.2 = (bf16[112,1536]{1,0:T(8,128)(2,1)}, bf16[112,1536]{1,0:T(8,128)(2,1)}, u32[]{:S(2)}, u32[]{:S(2)}) collective-permute-start(bf16[112,1536]{1,0:T(8,128)(2,1)} %get-tuple-element.20), channel_id=1, source_target_pairs={{0,1},{1,0},{2,3},{3,2},{4,5},{5,4},{6,7},{7,6},{8,9},{9,8},{10,11... | collective-permute-start | bytes 1032200 | tf_op jit(solution)/shard_map/ppermute | solution.py:651
  88.4 11.2 %collective-permute-start.3 = (bf16[112,1536]{1,0:T(8,128)(2,1)}, bf16[112,1536]{1,0:T(8,128)(2,1)}, u32[]{:S(2)}, u32[]{:S(2)}) collective-permute-start(bf16[112,1536]{1,0:T(8,128)(2,1)} %get-tuple-element.21), channel_id=1, source_target_pairs={{0,4},{1,5},{2,6},{3,7},{4,0},{5,1},{6,2},{7,3},{8,12},{9,13},{10,... | collective-permute-start | bytes 1032200 | tf_op jit(solution)/shard_map/ppermute | solution.py:651
  90.2 8.9 %copy-start.1 = (bf16[112,1536]{1,0:T(8,128)(2,1)}, bf16[112,1536]{1,0:T(8,128)(2,1)S(1)}, u32[]{:S(2)}) copy-start(bf16[112,1536]{1,0:T(8,128)(2,1)S(1)} %collective-permute-done.5.refs_5_) | copy-start | bytes 1032196
  90.2 15.9 %collective-permute-start.4 = (bf16[112,1536]{1,0:T(8,128)(2,1)}, bf16[112,1536]{1,0:T(8,128)(2,1)}, u32[]{:S(2)}, u32[]{:S(2)}) collective-permute-start(bf16[112,1536]{1,0:T(8,128)(2,1)} %get-tuple-element.22), channel_id=1, source_target_pairs={{0,5},{1,4},{2,7},{3,6},{4,1},{5,0},{6,3},{7,2},{8,13},{9,12},{10,... | collective-permute-start | bytes 1032200 | tf_op jit(solution)/shard_map/ppermute | solution.py:651
  99.1 7.0 %copy-start.2 = (bf16[112,1536]{1,0:T(8,128)(2,1)}, bf16[112,1536]{1,0:T(8,128)(2,1)S(1)}, u32[]{:S(2)}) copy-start(bf16[112,1536]{1,0:T(8,128)(2,1)S(1)} %collective-permute-done.6.refs_6_) | copy-start | bytes 1032196
  99.1 0.8 copy-start.3
  106.1 1.5 copy-start
where the time goes:
time: 174 us; the launch traced here: 171 us
  Pallas kernels  144 us (83%)
  starting transfers between devices  14.6 us (8%)
  waiting for transfers between devices  6.66 us (4%)
  local copies, waits for them, and re-layouts  3.79 us (2%)
    pallas_call x1, Pallas kernels, solve(): pl.pallas_call(solve_kernel, in_specs=[pl.BlockSpec(memory_space=pltpu.SM...  63.7 us
    pallas_call x2, Pallas kernels, more_planes(): pl.pallas_call(functools.partial(more_planes_kernel, depth=depth, flips=f...  41.1 us
    pallas_call x1, Pallas kernels, first_planes(): pl.pallas_call(functools.partial(first_planes_kernel, depth=depth, count=...  31.3 us
    pallas_call x1, Pallas kernels, fold(): pl.pallas_call(fold_kernel, grid=(depth // 2,), in_specs=[pl.BlockSpec((2...  8.24 us
    ppermute x6, waiting for transfers between devices, pairwise(): lax.ppermute(piece, 'wide', [(i, i ^ flip) for i in range(WIDE)])  6.65 us
    ppermute x1, starting transfers between devices, body(): high = lax.ppermute(forcing[:, :HALO], 'wide', backward)  4.28 us
    ppermute x6, starting transfers between devices, pairwise(): lax.ppermute(piece, 'wide', [(i, i ^ flip) for i in range(WIDE)])  4.19 us
    all_to_all x1, starting transfers between devices, body(): lax.all_to_all(own.reshape(8, padded, LEN_Y), 'wide', 0, 0, axis_index_gr...  3.82 us
  transfers between devices with their start and end apart: 9, of which 2 were waited for; matrix products, arithmetic and copies ran while one was open for 1% of the time, Pallas kernels for 29%

commit v1 on v0

--- a/solution.py
+++ b/solution.py
@@ -131,7 +131,7 @@
 DEPTH = 16
 HALO = ITERS - 1
 PARTS = 4
-UNROLL = 2
+UNROLL = 4
 TILE = 16
 FOLD = 16
 VMEM_LIMIT = 60 << 20
@@ -434,8 +434,8 @@
 
 
 def solve_kernel(scalars, slot_modes, forcing, block, *refs):
-    planes = refs[:-12]
-    out_ref, k_ref, f_ref, p_two, p_three, b_two, b_three, natural, stage, turned, sems, sem_out = refs[-12:]
+    planes = refs[:-11]
+    out_ref, k_ref, f_ref, p_two, p_three, b_two, b_three, stage, turned, sems, sem_out = refs[-11:]
     modes = block.shape[0]
     depth, padded, _ = k_ref.shape
     count = out_ref.shape[1]
@@ -523,21 +523,29 @@
                     flow_w = (k + below(k_ref, z, j)) * (p - below(src, z, j))
                     outs.append((flow_x + flow_w) + ((flow_y - left) + (flow_z - flows_z[j])))
                     next_flows.append(flow_z)
+                return next_flows, outs
+
+            def keep(z, outs):
                 for j in range(blocks):
-                    store(z, i, j, at, outs[j].astype(jnp.float32), factor)
-                return next_flows
+                    store(z, j, at, outs[j].astype(jnp.float32), factor)
+
+            def levels(first, flows_z):
+                found = []
+                for u in range(UNROLL):
+                    z = first + u
+                    flows_z, outs = level(z, isinstance(z, int) and z == depth - 1, flows_z)
+                    found.append(outs)
+                for u, outs in enumerate(found):
+                    keep(first + u, outs)
+                return flows_z
 
             def group(g, flows_z):
-                for u in range(UNROLL):
-                    flows_z = level(g * UNROLL + u, False, flows_z)
-                return flows_z
+                return levels(g * UNROLL, flows_z)
 
             flows = [-k_ref[0, at, cols(j)] * src[0, at, cols(j)] for j in range(blocks)]
             groups = depth // UNROLL - 1
             flows = lax.fori_loop(0, groups, group, flows)
-            for u in range(UNROLL):
-                z = groups * UNROLL + u
-                flows = level(z, z == depth - 1, flows)
+            levels(groups * UNROLL, flows)
 
         def plain(step):
             def load(ref, z, j, i):
@@ -565,29 +573,30 @@
 
     (a1, b1), (a2, b2), (a3, b3) = chebyshev()
 
-    def store_one(z, i, j, at, out, factor):
+    def store_one(z, j, at, out, factor):
         source = f_ref[z, at, cols(j)].astype(jnp.float32)
         value = ((1.0 + a1) / THETA + b1) * source - (0.5 * b1 / THETA * factor) * out
         p_two[z, at, cols(j)] = value
         b_two[z, at, cols(j)] = value.astype(jnp.bfloat16)
 
-    def store_two(z, i, j, at, out, factor):
+    def store_two(z, j, at, out, factor):
         source = f_ref[z, at, cols(j)].astype(jnp.float32)
         value = (1.0 + a2) * p_two[z, at, cols(j)] + (b2 - a2 / THETA) * source - (0.5 * b2 * factor) * out
         p_three[z, at, cols(j)] = value
         b_three[z, at, cols(j)] = value.astype(jnp.bfloat16)
 
-    def store_three(z, i, j, at, out, factor):
+    def store_three(z, j, at, out, factor):
         source = f_ref[z, at, cols(j)].astype(jnp.float32)
         old = (1.0 + a3) * p_three[z, at, cols(j)] - a3 * p_two[z, at, cols(j)]
-        value = old + (b3 * source - 0.5 * b3 * out)
-        for n in range(FOLD // 8):
-            to = pl.ds(i + 8 - HALO + 8 * n * tiles, 8, stride=tiles)
-            natural[z * blocks + j, to, :] = value[8 * n : 8 * n + 8]
+        b_two[z, at, cols(j)] = (old + (b3 * source - 0.5 * b3 * out)).astype(jnp.bfloat16)
 
     sweep(f_ref, store_one)
     sweep(b_two, store_two)
     sweep(b_three, store_three)
+
+    shape = (count, padded)
+    place = folded_row(lax.broadcasted_iota(jnp.int32, shape, 1), tiles)
+    unfold = (lax.broadcasted_iota(jnp.int32, shape, 0) + HALO == place).astype(jnp.bfloat16)
 
     def leave(z, slot):
         return pltpu.make_async_copy(turned.at[slot], out_ref.at[z], sem_out.at[slot])
@@ -596,8 +605,10 @@
         slot = z % 2
         if z > 1:
             leave(z - 2, slot).wait()
-        for j in range(blocks):
-            turned[slot, :, cols(j)] = natural[z * blocks + j, 8 : 8 + count, :].astype(jnp.bfloat16)
+        for n in range(0, LEN_Y, 512):
+            turned[slot, :, n : n + 512] = jnp.dot(
+                unfold, b_two[z, :, n : n + 512], preferred_element_type=jnp.float32
+            ).astype(jnp.bfloat16)
         leave(z, slot).start()
     for z in (depth - 2, depth - 1):
         leave(z, z % 2).wait()
@@ -621,7 +632,6 @@
             whole,
             narrow,
             narrow,
-            pltpu.VMEM((depth * LEN_Y // 128, padded + 8, 128), jnp.float32),
             pltpu.VMEM((2, depth, FOLD, LEN_Y), jnp.bfloat16),
             pltpu.VMEM((2, count, LEN_Y), jnp.bfloat16),
             pltpu.SemaphoreType.DMA((3, 1 + len(planes))),

time: 174 us -> 169 us (0.971)
  Pallas kernels: 144 us -> 140 us
    pallas_call x1, Pallas kernels: 63.7 us -> 59.2 us  [solve(): pl.pallas_call(solve_kernel, in_specs=[pl.BlockSpec(memory_space=pltpu.SM...]
  transfers between devices with their start and end apart: 9 -> 9, of which waited for: 2 -> 2; matrix products, arithmetic and copies ran while one was open for 1% -> 2% of each run, Pallas kernels for 29% -> 30%
where the time goes in v1:
time: 169 us; the launch traced here: 167 us
  Pallas kernels  140 us (83%)
  starting transfers between devices  14.6 us (9%)
  waiting for transfers between devices  6.66 us (4%)
  local copies, waits for them, and re-layouts  3.79 us (2%)
    pallas_call x1, Pallas kernels, solve(): pl.pallas_call(solve_kernel, in_specs=[pl.BlockSpec(memory_space=pltpu.SM...  59.2 us
    pallas_call x2, Pallas kernels, more_planes(): pl.pallas_call(functools.partial(more_planes_kernel, depth=depth, flips=f...  41.1 us
    pallas_call x1, Pallas kernels, first_planes(): pl.pallas_call(functools.partial(first_planes_kernel, depth=depth, count=...  31.3 us
    pallas_call x1, Pallas kernels, fold(): pl.pallas_call(fold_kernel, grid=(depth // 2,), in_specs=[pl.BlockSpec((2...  8.24 us
    ppermute x6, waiting for transfers between devices, pairwise(): lax.ppermute(piece, 'wide', [(i, i ^ flip) for i in range(WIDE)])  6.65 us
    ppermute x1, starting transfers between devices, body(): high = lax.ppermute(forcing[:, :HALO], 'wide', backward)  4.28 us
    ppermute x6, starting transfers between devices, pairwise(): lax.ppermute(piece, 'wide', [(i, i ^ flip) for i in range(WIDE)])  4.19 us
    all_to_all x1, starting transfers between devices, body(): lax.all_to_all(own.reshape(8, padded, LEN_Y), 'wide', 0, 0, axis_index_gr...  3.82 us
  transfers between devices with their start and end apart: 9, of which 2 were waited for; matrix products, arithmetic and copies ran while one was open for 2% of the time, Pallas kernels for 30%

profile of v1, /device:TPU:18, one launch (start us, length us, event | category | flops | bytes accessed | tf_op | source)
XLA Modules:
  0.0 167.0 jit_solution(5934917387895087840)
XLA Ops:
  0.7 0.6 pad_add_fusion.scalars
  1.3 31.3 %first_planes.1 = (bf16[896,1536]{1,0:T(8,128)(2,1)}, bf16[1536,1536]{1,0:T(8,128)(2,1)}, bf16[896,1536]{1,0:T(8,128)(2,1)}) custom-call(s32[2]{0:T(128)} %pad_add_fusion.scalars), custom_call_target="tpu_custom_call" | custom-call | flops 24999999488 | bytes 8000000 | tf_op jit(solution)/shard_map/first_planes/pallas_call | solution.py:310
  32.5 3.8 %all-to-all-start = ((bf16[8,112,1536]{2,1,0:T(8,128)(2,1)}), bf16[8,112,1536]{2,1,0:T(8,128)(2,1)S(1)}, u32[]{:S(2)}, u32[]{:S(2)}) async-start(bf16[8,112,1536]{2,1,0:T(8,128)(2,1)} %bitcast.4), calls=%async_computation | async-start | bytes 5505024 | tf_op jit(solution)/shard_map/all_to_all | solution.py:653
  36.4 20.5 %more_planes.3 = (bf16[112,1536]{1,0:T(8,128)(2,1)}, bf16[112,1536]{1,0:T(8,128)(2,1)}, bf16[112,1536]{1,0:T(8,128)(2,1)}, bf16[112,1536]{1,0:T(8,128)(2,1)}) custom-call(s32[2]{0:T(128)} %pad_add_fusion.scalars, bf16[1536,1536]{1,0:T(8,128)(2,1)} %get-tuple-element.17.basis_in, bf16[896,1536]{1,0:T(8,128)(2,1)} %get-tuple-element.18.folded_in), custom_call_target="tpu_custom_call" | custom-call | flops 20000000000 | bytes 8000000 | tf_op jit(solution)/shard_map/more_planes/pallas_call | solution.py:361
  56.9 0.6 collective-permute-start.5
  57.5 1.7 %collective-permute-start.6 = (bf16[112,1536]{1,0:T(8,128)(2,1)}, bf16[112,1536]{1,0:T(8,128)(2,1)S(1)}, u32[]{:S(2)}, u32[]{:S(2)}) collective-permute-start(bf16[112,1536]{1,0:T(8,128)(2,1)} %get-tuple-element.25), channel_id=1, source_target_pairs={{0,2},{1,3},{2,0},{3,1},{4,6},{5,7},{6,4},{7,5},{8,10},{9,11},{10,... | collective-permute-start | bytes 1032200 | tf_op jit(solution)/shard_map/ppermute | solution.py:661
  59.2 1.9 %fusion.2 = (bf16[16,3,1536]{2,1,0:T(4,128)(2,1)S(1)}, bf16[16,3,1536]{2,1,0:T(4,128)(2,1)}) fusion(bf16[16,96,1536]{2,1,0:T(8,128)(2,1)} %f_ref.1), kind=kLoop, calls=%fused_computation.10 | loop fusion | bytes 589824 | tf_op jit(solution)/shard_map/slice | solution.py:672
  61.1 2.4 %collective-permute-start = (bf16[16,3,1536]{2,1,0:T(4,128)(2,1)}, bf16[16,3,1536]{2,1,0:T(4,128)(2,1)}, u32[]{:S(2)}, u32[]{:S(2)}) collective-permute-start(bf16[16,3,1536]{2,1,0:T(4,128)(2,1)} %get-tuple-element.28), channel_id=1, source_target_pairs={{0,1},{1,2},{2,3},{3,4},{4,5},{5,6},{6,7},{7,8},{8,9},{9,10},{10,1... | collective-permute-start | bytes 442376 | tf_op jit(solution)/shard_map/ppermute | solution.py:671
  63.5 4.3 %collective-permute-start.1 = (bf16[16,3,1536]{2,1,0:T(4,128)(2,1)S(1)}, bf16[16,3,1536]{2,1,0:T(4,128)(2,1)}, u32[]{:S(2)}, u32[]{:S(2)}) collective-permute-start(bf16[16,3,1536]{2,1,0:T(4,128)(2,1)S(1)} %get-tuple-element.27), channel_id=1, source_target_pairs={{1,0},{2,1},{3,2},{4,3},{5,4},{6,5},{7,6},{8,7},{9,8},{10,9},{11,1... | collective-permute-start | bytes 442376 | tf_op jit(solution)/shard_map/ppermute | solution.py:672
  67.8 20.5 %more_planes.2 = (bf16[112,1536]{1,0:T(8,128)(2,1)}, bf16[112,1536]{1,0:T(8,128)(2,1)}, bf16[112,1536]{1,0:T(8,128)(2,1)}, bf16[112,1536]{1,0:T(8,128)(2,1)}) custom-call(s32[2]{0:T(128)} %pad_add_fusion.scalars, bf16[1536,1536]{1,0:T(8,128)(2,1)} %get-tuple-element.17.basis_in, bf16[896,1536]{1,0:T(8,128)(2,1)} %get-tuple-element.18.folded_in), custom_call_target="tpu_custom_call" | custom-call | flops 20000000000 | bytes 8000000 | tf_op jit(solution)/shard_map/more_planes/pallas_call | solution.py:361
  88.3 0.0 collective-permute-done.low_ref
  88.3 0.1 collective-permute-start.2
  88.4 1.8 %collective-permute-start.3 = (bf16[112,1536]{1,0:T(8,128)(2,1)}, bf16[112,1536]{1,0:T(8,128)(2,1)}, u32[]{:S(2)}, u32[]{:S(2)}) collective-permute-start(bf16[112,1536]{1,0:T(8,128)(2,1)} %get-tuple-element.21), channel_id=1, source_target_pairs={{0,4},{1,5},{2,6},{3,7},{4,0},{5,1},{6,2},{7,3},{8,12},{9,13},{10,... | collective-permute-start | bytes 1032200 | tf_op jit(solution)/shard_map/ppermute | solution.py:661
  90.2 0.0 collective-permute-done.5.refs_5_
  90.2 0.1 collective-permute-start.4
  90.3 0.6 compare_select_fusion.slot_modes
  90.9 8.2 %fold.1.forcing = bf16[16,112,1536]{2,1,0:T(8,128)(2,1)} custom-call(bf16[16,96,1536]{2,1,0:T(8,128)(2,1)} %f_ref.1, bf16[16,3,1536]{2,1,0:T(4,128)(2,1)} %collective-permute-done.low_ref, bf16[16,3,1536]{2,1,0:T(4,128)(2,1)} %collective-permute-done.1.high_ref), custom_call_target="tpu_custom_call" | custom-call | flops 1300000000 | bytes 10000000 | tf_op jit(solution)/shard_map/fold/pallas_call | solution.py:408
  99.1 0.0 collective-permute-done.7.refs_7_
  99.2 0.5 collective-permute-done.3.refs_2_
  99.7 0.3 copy-done.3
  99.9 6.2 %collective-permute-done.4.refs_3_ = bf16[112,1536]{1,0:T(8,128)(2,1)} collective-permute-done((bf16[112,1536]{1,0:T(8,128)(2,1)}, bf16[112,1536]{1,0:T(8,128)(2,1)}, u32[]{:S(2)}, u32[]{:S(2)}) %collective-permute-start.4) | collective-permute-done | bytes 344096 | tf_op jit(solution)/shard_map/ppermute | solution.py:661
  106.1 0.0 all-to-all-done.block
  106.1 1.5 copy-done
  107.7 59.2 %solve.1 = bf16[16,96,1536]{2,1,0:T(8,128)(2,1)} custom-call(s32[2]{0:T(128)} %pad_add_fusion.scalars, s32[1,256]{1,0:T(1,128)} %compare_select_fusion.slot_modes, bf16[16,112,1536]{2,1,0:T(8,128)(2,1)} %fold.1.forcing, bf16[8,112,1536]{2,1,0:T(8,128)(2,1)} %copy-done, bf16[112,1536]{1,0:T(8,128)(2,1)} %get-tuple-element.19.refs_0_, ...), custom_call_target="tpu_custom_call" | custom-call | tf_op jit(solution)/shard_map/solve/pallas_call | solution.py:622
  (10 shorter events, 0.0 us)
Async XLA Ops:
  32.5 73.6 %all-to-all-start = ((bf16[8,112,1536]{2,1,0:T(8,128)(2,1)}), bf16[8,112,1536]{2,1,0:T(8,128)(2,1)S(1)}, u32[]{:S(2)}, u32[]{:S(2)}) async-start(bf16[8,112,1536]{2,1,0:T(8,128)(2,1)} %bitcast.4), calls=%async_computation | async-start | bytes 5505024 | tf_op jit(solution)/shard_map/all_to_all | solution.py:653
  56.9 33.3 %collective-permute-start.5 = (bf16[112,1536]{1,0:T(8,128)(2,1)}, bf16[112,1536]{1,0:T(8,128)(2,1)S(1)}, u32[]{:S(2)}, u32[]{:S(2)}) collective-permute-start(bf16[112,1536]{1,0:T(8,128)(2,1)} %get-tuple-element.24), channel_id=1, source_target_pairs={{0,1},{1,0},{2,3},{3,2},{4,5},{5,4},{6,7},{7,6},{8,9},{9,8},{10,11... | collective-permute-start | bytes 1032200 | tf_op jit(solution)/shard_map/ppermute | solution.py:661
  57.5 41.6 %collective-permute-start.6 = (bf16[112,1536]{1,0:T(8,128)(2,1)}, bf16[112,1536]{1,0:T(8,128)(2,1)S(1)}, u32[]{:S(2)}, u32[]{:S(2)}) collective-permute-start(bf16[112,1536]{1,0:T(8,128)(2,1)} %get-tuple-element.25), channel_id=1, source_target_pairs={{0,2},{1,3},{2,0},{3,1},{4,6},{5,7},{6,4},{7,5},{8,10},{9,11},{10,... | collective-permute-start | bytes 1032200 | tf_op jit(solution)/shard_map/ppermute | solution.py:661
  59.2 40.0 %collective-permute-start.7 = (bf16[112,1536]{1,0:T(8,128)(2,1)}, bf16[112,1536]{1,0:T(8,128)(2,1)S(1)}, u32[]{:S(2)}, u32[]{:S(2)}) collective-permute-start(bf16[112,1536]{1,0:T(8,128)(2,1)} %get-tuple-element.26), channel_id=1, source_target_pairs={{0,3},{1,2},{2,1},{3,0},{4,7},{5,6},{6,5},{7,4},{8,11},{9,10},{10,... | collective-permute-start | bytes 1032200 | tf_op jit(solution)/shard_map/ppermute | solution.py:661
  61.1 27.2 %collective-permute-start = (bf16[16,3,1536]{2,1,0:T(4,128)(2,1)}, bf16[16,3,1536]{2,1,0:T(4,128)(2,1)}, u32[]{:S(2)}, u32[]{:S(2)}) collective-permute-start(bf16[16,3,1536]{2,1,0:T(4,128)(2,1)} %get-tuple-element.28), channel_id=1, source_target_pairs={{0,1},{1,2},{2,3},{3,4},{4,5},{5,6},{6,7},{7,8},{8,9},{9,10},{10,1... | collective-permute-start | bytes 442376 | tf_op jit(solution)/shard_map/ppermute | solution.py:671
  63.5 24.9 %collective-permute-start.1 = (bf16[16,3,1536]{2,1,0:T(4,128)(2,1)S(1)}, bf16[16,3,1536]{2,1,0:T(4,128)(2,1)}, u32[]{:S(2)}, u32[]{:S(2)}) collective-permute-start(bf16[16,3,1536]{2,1,0:T(4,128)(2,1)S(1)} %get-tuple-element.27), channel_id=1, source_target_pairs={{1,0},{2,1},{3,2},{4,3},{5,4},{6,5},{7,6},{8,7},{9,8},{10,9},{11,1... | collective-permute-start | bytes 442376 | tf_op jit(solution)/shard_map/ppermute | solution.py:672
  88.3 10.8 %collective-permute-start.2 = (bf16[112,1536]{1,0:T(8,128)(2,1)}, bf16[112,1536]{1,0:T(8,128)(2,1)}, u32[]{:S(2)}, u32[]{:S(2)}) collective-permute-start(bf16[112,1536]{1,0:T(8,128)(2,1)} %get-tuple-element.20), channel_id=1, source_target_pairs={{0,1},{1,0},{2,3},{3,2},{4,5},{5,4},{6,7},{7,6},{8,9},{9,8},{10,11... | collective-permute-start | bytes 1032200 | tf_op jit(solution)/shard_map/ppermute | solution.py:661
  88.4 11.2 %collective-permute-start.3 = (bf16[112,1536]{1,0:T(8,128)(2,1)}, bf16[112,1536]{1,0:T(8,128)(2,1)}, u32[]{:S(2)}, u32[]{:S(2)}) collective-permute-start(bf16[112,1536]{1,0:T(8,128)(2,1)} %get-tuple-element.21), channel_id=1, source_target_pairs={{0,4},{1,5},{2,6},{3,7},{4,0},{5,1},{6,2},{7,3},{8,12},{9,13},{10,... | collective-permute-start | bytes 1032200 | tf_op jit(solution)/shard_map/ppermute | solution.py:661
  90.2 8.9 %copy-start.1 = (bf16[112,1536]{1,0:T(8,128)(2,1)}, bf16[112,1536]{1,0:T(8,128)(2,1)S(1)}, u32[]{:S(2)}) copy-start(bf16[112,1536]{1,0:T(8,128)(2,1)S(1)} %collective-permute-done.5.refs_5_) | copy-start | bytes 1032196
  90.2 15.9 %collective-permute-start.4 = (bf16[112,1536]{1,0:T(8,128)(2,1)}, bf16[112,1536]{1,0:T(8,128)(2,1)}, u32[]{:S(2)}, u32[]{:S(2)}) collective-permute-start(bf16[112,1536]{1,0:T(8,128)(2,1)} %get-tuple-element.22), channel_id=1, source_target_pairs={{0,5},{1,4},{2,7},{3,6},{4,1},{5,0},{6,3},{7,2},{8,13},{9,12},{10,... | collective-permute-start | bytes 1032200 | tf_op jit(solution)/shard_map/ppermute | solution.py:661
  99.1 7.0 %copy-start.2 = (bf16[112,1536]{1,0:T(8,128)(2,1)}, bf16[112,1536]{1,0:T(8,128)(2,1)S(1)}, u32[]{:S(2)}) copy-start(bf16[112,1536]{1,0:T(8,128)(2,1)S(1)} %collective-permute-done.6.refs_6_) | copy-start | bytes 1032196
  99.1 0.8 copy-start.3
  106.1 1.5 copy-start

commit v2 on v1

--- a/solution.py
+++ b/solution.py
@@ -338,14 +338,19 @@
     return depth // 2 + 4 * color + 2 * (index & 1)
 
 
-def more_planes_kernel(scalars, basis_in, folded_in, *refs, depth, flips, offset):
+def beside_bit(core, offset):
+    return 4 >> (core ^ offset)
+
+
+def more_planes_kernel(scalars, basis_in, folded_in, *refs, depth, offset):
     out_refs = refs[:PARTS]
     basis, left, coef, rows, sem = refs[PARTS:]
     size = out_refs[0].shape[0]
     key, index = scalars[0], scalars[1]
     mode = shared_mode(index, depth) + offset
     copies = [pltpu.make_async_copy(basis_in, basis, sem.at[PARTS])]
-    for n, flip in enumerate(flips):
+    bit = beside_bit(index & 1, offset)
+    for n, flip in enumerate((0, 1, bit, bit ^ 1)):
         source = folded_in.at[pl.ds(pl.multiple_of((index & 7 ^ flip) * size, size), size), :]
         copies.append(pltpu.make_async_copy(source, left.at[pl.ds(n * size, size), :], sem.at[n]))
     for copy in copies:
@@ -356,10 +361,10 @@
     transform_into(out_refs, left, coef, rows, basis)
 
 
-def more_planes(scalars, basis, folded, depth, size, flips, offset):
+def more_planes(scalars, basis, folded, depth, size, offset):
     anywhere = pl.BlockSpec(memory_space=pl.ANY)
     return pl.pallas_call(
-        functools.partial(more_planes_kernel, depth=depth, flips=flips, offset=offset),
+        functools.partial(more_planes_kernel, depth=depth, offset=offset),
         in_specs=[pl.BlockSpec(memory_space=pltpu.SMEM), anywhere, anywhere],
         out_specs=[pl.BlockSpec(memory_space=pltpu.VMEM)] * PARTS,
         out_shape=[jax.ShapeDtypeStruct((size, LEN_Y), jnp.bfloat16)] * PARTS,
@@ -434,8 +439,8 @@
 
 
 def solve_kernel(scalars, slot_modes, forcing, block, *refs):
-    planes = refs[:-11]
-    out_ref, k_ref, f_ref, p_two, p_three, b_two, b_three, stage, turned, sems, sem_out = refs[-11:]
+    planes = refs[:-12]
+    out_ref, k_ref, y_ref, f_ref, p_two, p_three, b_two, b_three, stage, turned, sems, sem_out = refs[-12:]
     modes = block.shape[0]
     depth, padded, _ = k_ref.shape
     count = out_ref.shape[1]
@@ -491,9 +496,24 @@
                 part = field[:, :, j * 128 - n : j * 128 - n + 128]
                 value = jnp.exp(1.5 * jnp.tanh(2.0 * part)) * keep[None]
                 k_ref[:, t * FOLD : t * FOLD + FOLD, cols(j)] = value.astype(jnp.bfloat16)
-    forcing_copy.wait()
     lane = lax.broadcasted_iota(jnp.int32, (FOLD, 128), 1)
     nothing = jnp.zeros((FOLD, 128), jnp.bfloat16)
+
+    def faces(g, carry):
+        at = pl.ds(pl.multiple_of(g // (depth // 4) * FOLD, FOLD), FOLD)
+        sums = []
+        for u in range(4):
+            z = g % (depth // 4) * 4 + u
+            here = [k_ref[z, at, cols(j)] for j in range(blocks)]
+            turns = [pltpu.roll(k, 127, 1) for k in here] + [nothing]
+            sums.append((z, [here[j] + jnp.where(lane == 127, turns[j + 1], turns[j]) for j in range(blocks)]))
+        for z, values in sums:
+            for j in range(blocks):
+                y_ref[z, at, cols(j)] = values[j]
+        return carry
+
+    lax.fori_loop(0, tiles * depth // 4, faces, 0)
+    forcing_copy.wait()
 
     def sweep(src, store):
         def tile(i, below, above):
@@ -506,12 +526,10 @@
                 k_all = [k_ref[z, at, cols(j)] for j in range(blocks)]
                 p_all = [src[z, at, cols(j)] for j in range(blocks)]
                 turns = [pltpu.roll(p, 127, 1) for p in p_all] + [nothing]
-                k_turns = [pltpu.roll(k, 127, 1) for k in k_all] + [nothing]
                 before = None
                 for j in range(blocks):
                     k, p = k_all[j], p_all[j]
-                    k_right = jnp.where(lane == 127, k_turns[j + 1], k_turns[j])
-                    flow_y = (k + k_right) * (p - jnp.where(lane == 127, turns[j + 1], turns[j]))
+                    flow_y = y_ref[z, at, cols(j)] * (p - jnp.where(lane == 127, turns[j + 1], turns[j]))
                     flow_turn = pltpu.roll(flow_y, 1, 1)
                     left = jnp.where(lane == 0, -k * p if before is None else before, flow_turn)
                     before = flow_turn
@@ -628,6 +646,7 @@
         scratch_shapes=[
             narrow,
             narrow,
+            narrow,
             whole,
             whole,
             narrow,
@@ -654,18 +673,21 @@
         own.reshape(8, padded, LEN_Y), "wide", 0, 0, axis_index_groups=groups, tiled=True
     )
 
-    def pairwise(offset, bit):
-        flips = (0, 1, bit, bit ^ 1)
-        out = more_planes(scalars, basis, folded, depth, padded, flips, offset)
-        return [out[0]] + [
-            lax.ppermute(piece, "wide", [(i, i ^ flip) for i in range(WIDE)])
-            for piece, flip in zip(out[1:], flips[1:])
+    def pairwise(offset):
+        out = more_planes(scalars, basis, folded, depth, padded, offset)
+        routes = [
+            [(i, i ^ 1) for i in range(WIDE)],
+            [(i, i ^ beside_bit(i & 1, offset)) for i in range(WIDE)],
+            [(i, i ^ beside_bit(i & 1, offset) ^ 1) for i in range(WIDE)],
         ]
-
-    planes = pairwise(0, 4) + pairwise(1, 2)
+        return [out[0]] + [lax.ppermute(piece, "wide", route) for piece, route in zip(out[1:], routes)]
+
+    planes = pairwise(0) + pairwise(1)
     slot = lax.broadcasted_iota(jnp.int32, (1, depth * FOLD), 1) // FOLD
-    flip = jnp.where(slot < 12, (slot & 1) ^ (slot & 2) << 1, (slot & 1) ^ (slot & 2))
-    slot_modes = jnp.where(slot < 8, slot, shared_mode(index ^ flip, depth) + (slot >= 12))
+    offset = (slot >= 12).astype(jnp.int32)
+    source = index ^ (slot & 1)
+    source = source ^ jnp.where((slot & 2) == 0, 0, beside_bit(source & 1, offset))
+    slot_modes = jnp.where(slot < 8, slot, shared_mode(source, depth) + offset)
     forward = [(i, i + 1) for i in range(WIDE - 1)]
     backward = [(target, source) for source, target in forward]
     low = lax.ppermute(forcing[:, -HALO:], "wide", forward)

time: 169 us -> 162 us (0.959)
  waiting for transfers between devices: 6.66 us -> 0.38 us
  Pallas kernels: 140 us -> 138 us
    ppermute x6, waiting for transfers between devices: 6.65 us -> 0.38 us  [pairwise(): lax.ppermute(piece, 'wide', route)]
    pallas_call x1, Pallas kernels: 59.2 us -> 57.4 us  [solve(): pl.pallas_call(solve_kernel, in_specs=[pl.BlockSpec(memory_space=pltpu.SM...]
  transfers between devices with their start and end apart: 9 -> 9, of which waited for: 2 -> 1; matrix products, arithmetic and copies ran while one was open for 2% -> 2% of each run, Pallas kernels for 30% -> 31%
where the time goes in v2:
time: 162 us; the launch traced here: 159 us
  Pallas kernels  138 us (85%)
  starting transfers between devices  14.6 us (9%)
  local copies, waits for them, and re-layouts  4.27 us (3%)
    pallas_call x1, Pallas kernels, solve(): pl.pallas_call(solve_kernel, in_specs=[pl.BlockSpec(memory_space=pltpu.SM...  57.4 us
    pallas_call x2, Pallas kernels, more_planes(): pl.pallas_call(functools.partial(more_planes_kernel, depth=depth, offset=...  41.1 us
    pallas_call x1, Pallas kernels, first_planes(): pl.pallas_call(functools.partial(first_planes_kernel, depth=depth, count=...  31.3 us
    pallas_call x1, Pallas kernels, fold(): pl.pallas_call(fold_kernel, grid=(depth // 2,), in_specs=[pl.BlockSpec((2...  8.24 us
    ppermute x1, starting transfers between devices, body(): high = lax.ppermute(forcing[:, :HALO], 'wide', backward)  4.31 us
    ppermute x6, starting transfers between devices, pairwise(): lax.ppermute(piece, 'wide', route)  4.18 us
    all_to_all x1, starting transfers between devices, body(): lax.all_to_all(own.reshape(8, padded, LEN_Y), 'wide', 0, 0, axis_index_gr...  3.82 us
  transfers between devices with their start and end apart: 9, of which 1 were waited for; matrix products, arithmetic and copies ran while one was open for 2% of the time, Pallas kernels for 31%

profile of v2, /device:TPU:18, one launch (start us, length us, event | category | flops | bytes accessed | tf_op | source)
XLA Modules:
  0.0 159.4 jit_solution(7631804850923562165)
XLA Ops:
  0.7 0.6 pad_add_fusion.scalars
  1.3 31.3 %first_planes.1 = (bf16[896,1536]{1,0:T(8,128)(2,1)}, bf16[1536,1536]{1,0:T(8,128)(2,1)}, bf16[896,1536]{1,0:T(8,128)(2,1)}) custom-call(s32[2]{0:T(128)} %pad_add_fusion.scalars), custom_call_target="tpu_custom_call" | custom-call | flops 24999999488 | bytes 8000000 | tf_op jit(solution)/shard_map/first_planes/pallas_call | solution.py:310
  32.5 3.8 %all-to-all-start = ((bf16[8,112,1536]{2,1,0:T(8,128)(2,1)}), bf16[8,112,1536]{2,1,0:T(8,128)(2,1)S(1)}, u32[]{:S(2)}, u32[]{:S(2)}) async-start(bf16[8,112,1536]{2,1,0:T(8,128)(2,1)} %bitcast.4), calls=%async_computation | async-start | bytes 5505024 | tf_op jit(solution)/shard_map/all_to_all | solution.py:672
  36.4 20.5 %more_planes.3 = (bf16[112,1536]{1,0:T(8,128)(2,1)}, bf16[112,1536]{1,0:T(8,128)(2,1)}, bf16[112,1536]{1,0:T(8,128)(2,1)}, bf16[112,1536]{1,0:T(8,128)(2,1)}) custom-call(s32[2]{0:T(128)} %pad_add_fusion.scalars, bf16[1536,1536]{1,0:T(8,128)(2,1)} %get-tuple-element.17.basis_in, bf16[896,1536]{1,0:T(8,128)(2,1)} %get-tuple-element.18.folded_in), custom_call_target="tpu_custom_call" | custom-call | flops 20000000000 | bytes 8000000 | tf_op jit(solution)/shard_map/more_planes/pallas_call | solution.py:366
  56.9 0.6 collective-permute-start.5
  57.5 1.7 %collective-permute-start.6 = (bf16[112,1536]{1,0:T(8,128)(2,1)}, bf16[112,1536]{1,0:T(8,128)(2,1)S(1)}, u32[]{:S(2)}, u32[]{:S(2)}) collective-permute-start(bf16[112,1536]{1,0:T(8,128)(2,1)} %get-tuple-element.25), channel_id=1, source_target_pairs={{0,2},{1,5},{2,0},{3,7},{4,6},{5,1},{6,4},{7,3},{8,10},{9,13},{10,... | collective-permute-start | bytes 1032200 | tf_op jit(solution)/shard_map/ppermute | solution.py:683
  59.2 1.1 collective-permute-start.7
  60.3 1.9 %fusion.1 = (bf16[16,3,1536]{2,1,0:T(4,128)(2,1)S(1)}, bf16[16,3,1536]{2,1,0:T(4,128)(2,1)}) fusion(bf16[16,96,1536]{2,1,0:T(8,128)(2,1)} %f_ref.1), kind=kLoop, calls=%fused_computation.9 | loop fusion | bytes 589824 | tf_op jit(solution)/shard_map/slice | solution.py:694
  62.2 2.3 %collective-permute-start = (bf16[16,3,1536]{2,1,0:T(4,128)(2,1)}, bf16[16,3,1536]{2,1,0:T(4,128)(2,1)}, u32[]{:S(2)}, u32[]{:S(2)}) collective-permute-start(bf16[16,3,1536]{2,1,0:T(4,128)(2,1)} %get-tuple-element.28), channel_id=1, source_target_pairs={{0,1},{1,2},{2,3},{3,4},{4,5},{5,6},{6,7},{7,8},{8,9},{9,10},{10,1... | collective-permute-start | bytes 442376 | tf_op jit(solution)/shard_map/ppermute | solution.py:693
  64.6 4.3 %collective-permute-start.1 = (bf16[16,3,1536]{2,1,0:T(4,128)(2,1)S(1)}, bf16[16,3,1536]{2,1,0:T(4,128)(2,1)}, u32[]{:S(2)}, u32[]{:S(2)}) collective-permute-start(bf16[16,3,1536]{2,1,0:T(4,128)(2,1)S(1)} %get-tuple-element.27), channel_id=1, source_target_pairs={{1,0},{2,1},{3,2},{4,3},{5,4},{6,5},{7,6},{8,7},{9,8},{10,9},{11,1... | collective-permute-start | bytes 442376 | tf_op jit(solution)/shard_map/ppermute | solution.py:694
  68.9 20.5 %more_planes.2 = (bf16[112,1536]{1,0:T(8,128)(2,1)}, bf16[112,1536]{1,0:T(8,128)(2,1)}, bf16[112,1536]{1,0:T(8,128)(2,1)}, bf16[112,1536]{1,0:T(8,128)(2,1)}) custom-call(s32[2]{0:T(128)} %pad_add_fusion.scalars, bf16[1536,1536]{1,0:T(8,128)(2,1)} %get-tuple-element.17.basis_in, bf16[896,1536]{1,0:T(8,128)(2,1)} %get-tuple-element.18.folded_in), custom_call_target="tpu_custom_call" | custom-call | flops 20000000000 | bytes 8000000 | tf_op jit(solution)/shard_map/more_planes/pallas_call | solution.py:366
  89.5 0.1 collective-permute-start.2
  89.5 0.6 collective-permute-start.3
  90.2 0.0 collective-permute-done.5.refs_5_
  90.2 0.1 collective-permute-start.4
  90.3 0.6 compare_select_fusion.slot_modes
  90.9 8.2 %fold.1.forcing = bf16[16,112,1536]{2,1,0:T(8,128)(2,1)} custom-call(bf16[16,96,1536]{2,1,0:T(8,128)(2,1)} %f_ref.1, bf16[16,3,1536]{2,1,0:T(4,128)(2,1)} %collective-permute-done.low_ref, bf16[16,3,1536]{2,1,0:T(4,128)(2,1)} %collective-permute-done.1.high_ref), custom_call_target="tpu_custom_call" | custom-call | flops 1300000000 | bytes 10000000 | tf_op jit(solution)/shard_map/fold/pallas_call | solution.py:413
  99.1 0.0 collective-permute-done.7.refs_7_
  99.2 0.0 collective-permute-done.2.refs_1_
  99.2 0.8 copy-done.3
  99.9 0.4 collective-permute-done.4.refs_3_
  100.3 0.0 all-to-all-done.block
  100.3 1.5 copy-done
  101.9 57.4 %solve.1 = bf16[16,96,1536]{2,1,0:T(8,128)(2,1)} custom-call(s32[2]{0:T(128)} %pad_add_fusion.scalars, s32[1,256]{1,0:T(1,128)} %compare_select_fusion.slot_modes, bf16[16,112,1536]{2,1,0:T(8,128)(2,1)} %fold.1.forcing, bf16[8,112,1536]{2,1,0:T(8,128)(2,1)} %copy-done, bf16[112,1536]{1,0:T(8,128)(2,1)} %get-tuple-element.19.refs_0_, ...), custom_call_target="tpu_custom_call" | custom-call | tf_op jit(solution)/shard_map/solve/pallas_call | solution.py:640
  (10 shorter events, 0.0 us)
Async XLA Ops:
  32.5 67.8 %all-to-all-start = ((bf16[8,112,1536]{2,1,0:T(8,128)(2,1)}), bf16[8,112,1536]{2,1,0:T(8,128)(2,1)S(1)}, u32[]{:S(2)}, u32[]{:S(2)}) async-start(bf16[8,112,1536]{2,1,0:T(8,128)(2,1)} %bitcast.4), calls=%async_computation | async-start | bytes 5505024 | tf_op jit(solution)/shard_map/all_to_all | solution.py:672
  56.9 33.3 %collective-permute-start.5 = (bf16[112,1536]{1,0:T(8,128)(2,1)}, bf16[112,1536]{1,0:T(8,128)(2,1)S(1)}, u32[]{:S(2)}, u32[]{:S(2)}) collective-permute-start(bf16[112,1536]{1,0:T(8,128)(2,1)} %get-tuple-element.24), channel_id=1, source_target_pairs={{0,1},{1,0},{2,3},{3,2},{4,5},{5,4},{6,7},{7,6},{8,9},{9,8},{10,11... | collective-permute-start | bytes 1032200 | tf_op jit(solution)/shard_map/ppermute | solution.py:683
  57.5 41.6 %collective-permute-start.6 = (bf16[112,1536]{1,0:T(8,128)(2,1)}, bf16[112,1536]{1,0:T(8,128)(2,1)S(1)}, u32[]{:S(2)}, u32[]{:S(2)}) collective-permute-start(bf16[112,1536]{1,0:T(8,128)(2,1)} %get-tuple-element.25), channel_id=1, source_target_pairs={{0,2},{1,5},{2,0},{3,7},{4,6},{5,1},{6,4},{7,3},{8,10},{9,13},{10,... | collective-permute-start | bytes 1032200 | tf_op jit(solution)/shard_map/ppermute | solution.py:683
  59.2 40.0 %collective-permute-start.7 = (bf16[112,1536]{1,0:T(8,128)(2,1)}, bf16[112,1536]{1,0:T(8,128)(2,1)S(1)}, u32[]{:S(2)}, u32[]{:S(2)}) collective-permute-start(bf16[112,1536]{1,0:T(8,128)(2,1)} %get-tuple-element.26), channel_id=1, source_target_pairs={{0,3},{1,4},{2,1},{3,6},{4,7},{5,0},{6,5},{7,2},{8,11},{9,12},{10,... | collective-permute-start | bytes 1032200 | tf_op jit(solution)/shard_map/ppermute | solution.py:683
  62.2 27.2 %collective-permute-start = (bf16[16,3,1536]{2,1,0:T(4,128)(2,1)}, bf16[16,3,1536]{2,1,0:T(4,128)(2,1)}, u32[]{:S(2)}, u32[]{:S(2)}) collective-permute-start(bf16[16,3,1536]{2,1,0:T(4,128)(2,1)} %get-tuple-element.28), channel_id=1, source_target_pairs={{0,1},{1,2},{2,3},{3,4},{4,5},{5,6},{6,7},{7,8},{8,9},{9,10},{10,1... | collective-permute-start | bytes 442376 | tf_op jit(solution)/shard_map/ppermute | solution.py:693
  64.6 24.9 %collective-permute-start.1 = (bf16[16,3,1536]{2,1,0:T(4,128)(2,1)S(1)}, bf16[16,3,1536]{2,1,0:T(4,128)(2,1)}, u32[]{:S(2)}, u32[]{:S(2)}) collective-permute-start(bf16[16,3,1536]{2,1,0:T(4,128)(2,1)S(1)} %get-tuple-element.27), channel_id=1, source_target_pairs={{1,0},{2,1},{3,2},{4,3},{5,4},{6,5},{7,6},{8,7},{9,8},{10,9},{11,1... | collective-permute-start | bytes 442376 | tf_op jit(solution)/shard_map/ppermute | solution.py:694
  89.5 9.7 %collective-permute-start.2 = (bf16[112,1536]{1,0:T(8,128)(2,1)}, bf16[112,1536]{1,0:T(8,128)(2,1)}, u32[]{:S(2)}, u32[]{:S(2)}) collective-permute-start(bf16[112,1536]{1,0:T(8,128)(2,1)} %get-tuple-element.20), channel_id=1, source_target_pairs={{0,1},{1,0},{2,3},{3,2},{4,5},{5,4},{6,7},{7,6},{8,9},{9,8},{10,11... | collective-permute-start | bytes 1032200 | tf_op jit(solution)/shard_map/ppermute | solution.py:683
  89.5 9.6 %collective-permute-start.3 = (bf16[112,1536]{1,0:T(8,128)(2,1)}, bf16[112,1536]{1,0:T(8,128)(2,1)}, u32[]{:S(2)}, u32[]{:S(2)}) collective-permute-start(bf16[112,1536]{1,0:T(8,128)(2,1)} %get-tuple-element.21), channel_id=1, source_target_pairs={{0,4},{1,3},{2,6},{3,1},{4,0},{5,7},{6,2},{7,5},{8,12},{9,11},{10,... | collective-permute-start | bytes 1032200 | tf_op jit(solution)/shard_map/ppermute | solution.py:683
  90.2 8.9 %copy-start.1 = (bf16[112,1536]{1,0:T(8,128)(2,1)}, bf16[112,1536]{1,0:T(8,128)(2,1)S(1)}, u32[]{:S(2)}) copy-start(bf16[112,1536]{1,0:T(8,128)(2,1)S(1)} %collective-permute-done.5.refs_5_) | copy-start | bytes 1032196
  90.2 10.1 %collective-permute-start.4 = (bf16[112,1536]{1,0:T(8,128)(2,1)}, bf16[112,1536]{1,0:T(8,128)(2,1)}, u32[]{:S(2)}, u32[]{:S(2)}) collective-permute-start(bf16[112,1536]{1,0:T(8,128)(2,1)} %get-tuple-element.22), channel_id=1, source_target_pairs={{0,5},{1,2},{2,7},{3,0},{4,1},{5,6},{6,3},{7,4},{8,13},{9,10},{10,... | collective-permute-start | bytes 1032200 | tf_op jit(solution)/shard_map/ppermute | solution.py:683
  99.1 1.2 copy-start.2
  99.1 0.8 copy-start.3
  100.3 1.5 copy-start

commit v3 on v2

--- a/solution.py
+++ b/solution.py
@@ -184,10 +184,23 @@
     lax.fori_loop(0, cos_out.shape[0] // 8, part, 0)
 
 
-def basis_into(out_ref, small, big):
+def angle_sums(out, first, second):
+    rows, length = second[0].shape
+    for m in range(out[0].shape[0] // rows):
+        for j in range(length // 128):
+            cols = slice(j * 128, (j + 1) * 128)
+            cos_a, sin_a = first[0][m : m + 1, cols], first[1][m : m + 1, cols]
+            cos_b, sin_b = second[0][:, cols], second[1][:, cols]
+            out[0][m * rows : (m + 1) * rows, cols] = cos_a * cos_b - sin_a * sin_b
+            out[1][m * rows : (m + 1) * rows, cols] = sin_a * cos_b + cos_a * sin_b
+
+
+def basis_into(out_ref, small, big, first, second):
     rows = small[0].shape[0]
     length = out_ref.shape[1]
-    angle_tables(*small, lambda r: 2 * r + 1, length, True)
+    angle_tables(*first, lambda m: 16 * m, length, True)
+    angle_tables(*second, lambda r: 2 * r + 1, length, False)
+    angle_sums(small, first, second)
     angle_tables(*big, lambda t: 2 * rows * t, length, False)
 
     def group(g, carry):
@@ -205,13 +218,12 @@
     lax.fori_loop(0, big[0].shape[0] // 8, group, 0)
 
 
-def folded_basis_into(out_ref, small, big, first_row, count, tiles):
+def folded_basis_into(out_ref, small, big, first, second, first_row, count, tiles):
     length = out_ref.shape[1]
 
-    def block_row(r):
-        return 2 * (first_row + r // FOLD * count - HALO + r % FOLD * tiles) + 1
-
-    angle_tables(*small, block_row, length, True)
+    angle_tables(*first, lambda d: 2 * (first_row + d * count - HALO) + 1, length, True)
+    angle_tables(*second, lambda r: 2 * tiles * r, length, False)
+    angle_sums(small, first, second)
     angle_tables(*big, lambda i: 2 * i, length, False)
 
     def device(d, carry):
@@ -279,15 +291,21 @@
 
 
 def first_planes_kernel(
-    scalars, out_ref, basis_out, folded_out, basis, folded, coef, rows, small_cos, small_sin, big_cos, big_sin, sem,
-    *, depth, count, tiles
+    scalars, out_ref, basis_out, folded_out, basis, folded, coef, rows, small_cos, small_sin, big_cos, big_sin,
+    one_cos, one_sin, two_cos, two_sin, sem, *, depth, count, tiles
 ):
     key, index = scalars[0], scalars[1]
-    basis_into(basis, (small_cos.at[pl.ds(0, 64)], small_sin.at[pl.ds(0, 64)]), (big_cos, big_sin))
+    first = (one_cos, one_sin)
+    second = (two_cos.at[pl.ds(0, 8)], two_sin.at[pl.ds(0, 8)])
+    basis_into(
+        basis, (small_cos.at[pl.ds(0, 64)], small_sin.at[pl.ds(0, 64)]), (big_cos, big_sin), first, second
+    )
     folded_basis_into(
         folded,
         (small_cos, small_sin),
         (big_cos.at[pl.ds(0, 8)], big_sin.at[pl.ds(0, 8)]),
+        first,
+        (two_cos, two_sin),
         (index >> 3) * (8 * count),
         count,
         tiles,
@@ -325,6 +343,10 @@
             pltpu.VMEM((8 * FOLD, LEN_X), jnp.float32),
             pltpu.VMEM((LEN_X // 64, LEN_X), jnp.float32),
             pltpu.VMEM((LEN_X // 64, LEN_X), jnp.float32),
+            pltpu.VMEM((8, LEN_X), jnp.float32),
+            pltpu.VMEM((8, LEN_X), jnp.float32),
+            pltpu.VMEM((FOLD, LEN_X), jnp.float32),
+            pltpu.VMEM((FOLD, LEN_X), jnp.float32),
             pltpu.SemaphoreType.DMA((2,)),
         ],
         compiler_params=pltpu.CompilerParams(vmem_limit_bytes=VMEM_LIMIT),

time: 162 us -> 161 us (level)
  no operation moved by 1% of the time
where the time goes in v3:
time: 161 us; the launch traced here: 158 us
  Pallas kernels  137 us (85%)
  starting transfers between devices  14.6 us (9%)
  local copies, waits for them, and re-layouts  4.27 us (3%)
    pallas_call x1, Pallas kernels, solve(): pl.pallas_call(solve_kernel, in_specs=[pl.BlockSpec(memory_space=pltpu.SM...  57.4 us
    pallas_call x2, Pallas kernels, more_planes(): pl.pallas_call(functools.partial(more_planes_kernel, depth=depth, offset=...  41.1 us
    pallas_call x1, Pallas kernels, first_planes(): pl.pallas_call(functools.partial(first_planes_kernel, depth=depth, count=...  29.9 us
    pallas_call x1, Pallas kernels, fold(): pl.pallas_call(fold_kernel, grid=(depth // 2,), in_specs=[pl.BlockSpec((2...  8.24 us
    ppermute x1, starting transfers between devices, body(): high = lax.ppermute(forcing[:, :HALO], 'wide', backward)  4.31 us
    ppermute x6, starting transfers between devices, pairwise(): lax.ppermute(piece, 'wide', route)  4.18 us
    all_to_all x1, starting transfers between devices, body(): lax.all_to_all(own.reshape(8, padded, LEN_Y), 'wide', 0, 0, axis_index_gr...  3.82 us
  transfers between devices with their start and end apart: 9, of which 1 were waited for; matrix products, arithmetic and copies ran while one was open for 2% of the time, Pallas kernels for 31%

profile of v3, /device:TPU:18, one launch (start us, length us, event | category | flops | bytes accessed | tf_op | source)
XLA Modules:
  0.0 158.0 jit_solution(13280261286347370420)
XLA Ops:
  0.7 0.6 pad_add_fusion.scalars
  1.3 29.9 %first_planes.1 = (bf16[896,1536]{1,0:T(8,128)(2,1)}, bf16[1536,1536]{1,0:T(8,128)(2,1)}, bf16[896,1536]{1,0:T(8,128)(2,1)}) custom-call(s32[2]{0:T(128)} %pad_add_fusion.scalars), custom_call_target="tpu_custom_call" | custom-call | flops 24999999488 | bytes 8000000 | tf_op jit(solution)/shard_map/first_planes/pallas_call | solution.py:328
  31.1 3.8 %all-to-all-start = ((bf16[8,112,1536]{2,1,0:T(8,128)(2,1)}), bf16[8,112,1536]{2,1,0:T(8,128)(2,1)S(1)}, u32[]{:S(2)}, u32[]{:S(2)}) async-start(bf16[8,112,1536]{2,1,0:T(8,128)(2,1)} %bitcast.4), calls=%async_computation | async-start | bytes 5505024 | tf_op jit(solution)/shard_map/all_to_all | solution.py:694
  35.0 20.5 %more_planes.3 = (bf16[112,1536]{1,0:T(8,128)(2,1)}, bf16[112,1536]{1,0:T(8,128)(2,1)}, bf16[112,1536]{1,0:T(8,128)(2,1)}, bf16[112,1536]{1,0:T(8,128)(2,1)}) custom-call(s32[2]{0:T(128)} %pad_add_fusion.scalars, bf16[1536,1536]{1,0:T(8,128)(2,1)} %get-tuple-element.17.basis_in, bf16[896,1536]{1,0:T(8,128)(2,1)} %get-tuple-element.18.folded_in), custom_call_target="tpu_custom_call" | custom-call | flops 20000000000 | bytes 8000000 | tf_op jit(solution)/shard_map/more_planes/pallas_call | solution.py:388
  55.5 0.6 collective-permute-start.5
  56.1 1.7 %collective-permute-start.6 = (bf16[112,1536]{1,0:T(8,128)(2,1)}, bf16[112,1536]{1,0:T(8,128)(2,1)S(1)}, u32[]{:S(2)}, u32[]{:S(2)}) collective-permute-start(bf16[112,1536]{1,0:T(8,128)(2,1)} %get-tuple-element.25), channel_id=1, source_target_pairs={{0,2},{1,5},{2,0},{3,7},{4,6},{5,1},{6,4},{7,3},{8,10},{9,13},{10,... | collective-permute-start | bytes 1032200 | tf_op jit(solution)/shard_map/ppermute | solution.py:705
  57.8 1.2 collective-permute-start.7
  58.9 1.9 %fusion.1 = (bf16[16,3,1536]{2,1,0:T(4,128)(2,1)S(1)}, bf16[16,3,1536]{2,1,0:T(4,128)(2,1)}) fusion(bf16[16,96,1536]{2,1,0:T(8,128)(2,1)} %f_ref.1), kind=kLoop, calls=%fused_computation.9 | loop fusion | bytes 589824 | tf_op jit(solution)/shard_map/slice | solution.py:716
  60.9 2.3 %collective-permute-start = (bf16[16,3,1536]{2,1,0:T(4,128)(2,1)}, bf16[16,3,1536]{2,1,0:T(4,128)(2,1)}, u32[]{:S(2)}, u32[]{:S(2)}) collective-permute-start(bf16[16,3,1536]{2,1,0:T(4,128)(2,1)} %get-tuple-element.28), channel_id=1, source_target_pairs={{0,1},{1,2},{2,3},{3,4},{4,5},{5,6},{6,7},{7,8},{8,9},{9,10},{10,1... | collective-permute-start | bytes 442376 | tf_op jit(solution)/shard_map/ppermute | solution.py:715
  63.2 4.3 %collective-permute-start.1 = (bf16[16,3,1536]{2,1,0:T(4,128)(2,1)S(1)}, bf16[16,3,1536]{2,1,0:T(4,128)(2,1)}, u32[]{:S(2)}, u32[]{:S(2)}) collective-permute-start(bf16[16,3,1536]{2,1,0:T(4,128)(2,1)S(1)} %get-tuple-element.27), channel_id=1, source_target_pairs={{1,0},{2,1},{3,2},{4,3},{5,4},{6,5},{7,6},{8,7},{9,8},{10,9},{11,1... | collective-permute-start | bytes 442376 | tf_op jit(solution)/shard_map/ppermute | solution.py:716
  67.5 20.5 %more_planes.2 = (bf16[112,1536]{1,0:T(8,128)(2,1)}, bf16[112,1536]{1,0:T(8,128)(2,1)}, bf16[112,1536]{1,0:T(8,128)(2,1)}, bf16[112,1536]{1,0:T(8,128)(2,1)}) custom-call(s32[2]{0:T(128)} %pad_add_fusion.scalars, bf16[1536,1536]{1,0:T(8,128)(2,1)} %get-tuple-element.17.basis_in, bf16[896,1536]{1,0:T(8,128)(2,1)} %get-tuple-element.18.folded_in), custom_call_target="tpu_custom_call" | custom-call | flops 20000000000 | bytes 8000000 | tf_op jit(solution)/shard_map/more_planes/pallas_call | solution.py:388
  88.1 0.1 collective-permute-start.2
  88.1 0.0 collective-permute-done.1.high_ref
  88.1 0.6 collective-permute-start.3
  88.8 0.0 collective-permute-done.5.refs_5_
  88.8 0.1 collective-permute-start.4
  88.9 0.6 compare_select_fusion.slot_modes
  89.5 8.2 %fold.1.forcing = bf16[16,112,1536]{2,1,0:T(8,128)(2,1)} custom-call(bf16[16,96,1536]{2,1,0:T(8,128)(2,1)} %f_ref.1, bf16[16,3,1536]{2,1,0:T(4,128)(2,1)} %collective-permute-done.low_ref, bf16[16,3,1536]{2,1,0:T(4,128)(2,1)} %collective-permute-done.1.high_ref), custom_call_target="tpu_custom_call" | custom-call | flops 1300000000 | bytes 10000000 | tf_op jit(solution)/shard_map/fold/pallas_call | solution.py:435
  97.7 0.0 collective-permute-done.7.refs_7_
  97.8 0.0 collective-permute-done.2.refs_1_
  97.8 0.8 copy-done.3
  98.6 0.4 collective-permute-done.4.refs_3_
  98.9 1.5 copy-done
  100.5 57.4 %solve.1 = bf16[16,96,1536]{2,1,0:T(8,128)(2,1)} custom-call(s32[2]{0:T(128)} %pad_add_fusion.scalars, s32[1,256]{1,0:T(1,128)} %compare_select_fusion.slot_modes, bf16[16,112,1536]{2,1,0:T(8,128)(2,1)} %fold.1.forcing, bf16[8,112,1536]{2,1,0:T(8,128)(2,1)} %copy-done, bf16[112,1536]{1,0:T(8,128)(2,1)} %get-tuple-element.19.refs_0_, ...), custom_call_target="tpu_custom_call" | custom-call | tf_op jit(solution)/shard_map/solve/pallas_call | solution.py:662
  (10 shorter events, 0.0 us)
Async XLA Ops:
  31.1 67.8 %all-to-all-start = ((bf16[8,112,1536]{2,1,0:T(8,128)(2,1)}), bf16[8,112,1536]{2,1,0:T(8,128)(2,1)S(1)}, u32[]{:S(2)}, u32[]{:S(2)}) async-start(bf16[8,112,1536]{2,1,0:T(8,128)(2,1)} %bitcast.4), calls=%async_computation | async-start | bytes 5505024 | tf_op jit(solution)/shard_map/all_to_all | solution.py:694
  55.5 33.3 %collective-permute-start.5 = (bf16[112,1536]{1,0:T(8,128)(2,1)}, bf16[112,1536]{1,0:T(8,128)(2,1)S(1)}, u32[]{:S(2)}, u32[]{:S(2)}) collective-permute-start(bf16[112,1536]{1,0:T(8,128)(2,1)} %get-tuple-element.24), channel_id=1, source_target_pairs={{0,1},{1,0},{2,3},{3,2},{4,5},{5,4},{6,7},{7,6},{8,9},{9,8},{10,11... | collective-permute-start | bytes 1032200 | tf_op jit(solution)/shard_map/ppermute | solution.py:705
  56.1 41.6 %collective-permute-start.6 = (bf16[112,1536]{1,0:T(8,128)(2,1)}, bf16[112,1536]{1,0:T(8,128)(2,1)S(1)}, u32[]{:S(2)}, u32[]{:S(2)}) collective-permute-start(bf16[112,1536]{1,0:T(8,128)(2,1)} %get-tuple-element.25), channel_id=1, source_target_pairs={{0,2},{1,5},{2,0},{3,7},{4,6},{5,1},{6,4},{7,3},{8,10},{9,13},{10,... | collective-permute-start | bytes 1032200 | tf_op jit(solution)/shard_map/ppermute | solution.py:705
  57.8 40.0 %collective-permute-start.7 = (bf16[112,1536]{1,0:T(8,128)(2,1)}, bf16[112,1536]{1,0:T(8,128)(2,1)S(1)}, u32[]{:S(2)}, u32[]{:S(2)}) collective-permute-start(bf16[112,1536]{1,0:T(8,128)(2,1)} %get-tuple-element.26), channel_id=1, source_target_pairs={{0,3},{1,4},{2,1},{3,6},{4,7},{5,0},{6,5},{7,2},{8,11},{9,12},{10,... | collective-permute-start | bytes 1032200 | tf_op jit(solution)/shard_map/ppermute | solution.py:705
  60.9 27.2 %collective-permute-start = (bf16[16,3,1536]{2,1,0:T(4,128)(2,1)}, bf16[16,3,1536]{2,1,0:T(4,128)(2,1)}, u32[]{:S(2)}, u32[]{:S(2)}) collective-permute-start(bf16[16,3,1536]{2,1,0:T(4,128)(2,1)} %get-tuple-element.28), channel_id=1, source_target_pairs={{0,1},{1,2},{2,3},{3,4},{4,5},{5,6},{6,7},{7,8},{8,9},{9,10},{10,1... | collective-permute-start | bytes 442376 | tf_op jit(solution)/shard_map/ppermute | solution.py:715
  63.2 24.9 %collective-permute-start.1 = (bf16[16,3,1536]{2,1,0:T(4,128)(2,1)S(1)}, bf16[16,3,1536]{2,1,0:T(4,128)(2,1)}, u32[]{:S(2)}, u32[]{:S(2)}) collective-permute-start(bf16[16,3,1536]{2,1,0:T(4,128)(2,1)S(1)} %get-tuple-element.27), channel_id=1, source_target_pairs={{1,0},{2,1},{3,2},{4,3},{5,4},{6,5},{7,6},{8,7},{9,8},{10,9},{11,1... | collective-permute-start | bytes 442376 | tf_op jit(solution)/shard_map/ppermute | solution.py:716
  88.1 9.7 %collective-permute-start.2 = (bf16[112,1536]{1,0:T(8,128)(2,1)}, bf16[112,1536]{1,0:T(8,128)(2,1)}, u32[]{:S(2)}, u32[]{:S(2)}) collective-permute-start(bf16[112,1536]{1,0:T(8,128)(2,1)} %get-tuple-element.20), channel_id=1, source_target_pairs={{0,1},{1,0},{2,3},{3,2},{4,5},{5,4},{6,7},{7,6},{8,9},{9,8},{10,11... | collective-permute-start | bytes 1032200 | tf_op jit(solution)/shard_map/ppermute | solution.py:705
  88.1 9.6 %collective-permute-start.3 = (bf16[112,1536]{1,0:T(8,128)(2,1)}, bf16[112,1536]{1,0:T(8,128)(2,1)}, u32[]{:S(2)}, u32[]{:S(2)}) collective-permute-start(bf16[112,1536]{1,0:T(8,128)(2,1)} %get-tuple-element.21), channel_id=1, source_target_pairs={{0,4},{1,3},{2,6},{3,1},{4,0},{5,7},{6,2},{7,5},{8,12},{9,11},{10,... | collective-permute-start | bytes 1032200 | tf_op jit(solution)/shard_map/ppermute | solution.py:705
  88.8 8.9 %copy-start.1 = (bf16[112,1536]{1,0:T(8,128)(2,1)}, bf16[112,1536]{1,0:T(8,128)(2,1)S(1)}, u32[]{:S(2)}) copy-start(bf16[112,1536]{1,0:T(8,128)(2,1)S(1)} %collective-permute-done.5.refs_5_) | copy-start | bytes 1032196
  88.8 10.1 %collective-permute-start.4 = (bf16[112,1536]{1,0:T(8,128)(2,1)}, bf16[112,1536]{1,0:T(8,128)(2,1)}, u32[]{:S(2)}, u32[]{:S(2)}) collective-permute-start(bf16[112,1536]{1,0:T(8,128)(2,1)} %get-tuple-element.22), channel_id=1, source_target_pairs={{0,5},{1,2},{2,7},{3,0},{4,1},{5,6},{6,3},{7,4},{8,13},{9,10},{10,... | collective-permute-start | bytes 1032200 | tf_op jit(solution)/shard_map/ppermute | solution.py:705
  97.7 1.2 copy-start.2
  97.7 0.8 copy-start.3
  98.9 1.5 copy-start

commit v4 on v3

--- a/solution.py
+++ b/solution.py
@@ -277,14 +277,14 @@
 
 
 def transform_into(out_refs, left_ref, coef_ref, rows_ref, basis_ref):
-    for n in range(0, LEN_Y, 256):
-        cols = slice(n, n + 256)
+    for n in range(0, LEN_Y, 512):
+        cols = slice(n, n + 512)
         rows_ref[:, cols] = jnp.dot(
             left_ref[...], coef_ref[:, cols], preferred_element_type=jnp.float32
         ).astype(jnp.bfloat16)
     size = rows_ref.shape[0] // len(out_refs)
-    for n in range(0, LEN_Y, 256):
-        cols = slice(n, n + 256)
+    for n in range(0, LEN_Y, 512):
+        cols = slice(n, n + 512)
         value = contract_last(rows_ref[...], basis_ref[cols, :])
         for m, out_ref in enumerate(out_refs):
             out_ref[:, cols] = value[m * size : (m + 1) * size].astype(jnp.bfloat16)

time: 161 us -> 161 us (level)
  no operation moved by 1% of the time
where the time goes in v4:
time: 161 us; the launch traced here: 158 us
  Pallas kernels  137 us (85%)
  starting transfers between devices  14.6 us (9%)
  local copies, waits for them, and re-layouts  4.27 us (3%)
    pallas_call x1, Pallas kernels, solve(): pl.pallas_call(solve_kernel, in_specs=[pl.BlockSpec(memory_space=pltpu.SM...  57.4 us
    pallas_call x2, Pallas kernels, more_planes(): pl.pallas_call(functools.partial(more_planes_kernel, depth=depth, offset=...  41.1 us
    pallas_call x1, Pallas kernels, first_planes(): pl.pallas_call(functools.partial(first_planes_kernel, depth=depth, count=...  29.9 us
    pallas_call x1, Pallas kernels, fold(): pl.pallas_call(fold_kernel, grid=(depth // 2,), in_specs=[pl.BlockSpec((2...  8.24 us
    ppermute x1, starting transfers between devices, body(): high = lax.ppermute(forcing[:, :HALO], 'wide', backward)  4.31 us
    ppermute x6, starting transfers between devices, pairwise(): lax.ppermute(piece, 'wide', route)  4.18 us
    all_to_all x1, starting transfers between devices, body(): lax.all_to_all(own.reshape(8, padded, LEN_Y), 'wide', 0, 0, axis_index_gr...  3.82 us
  transfers between devices with their start and end apart: 9, of which 1 were waited for; matrix products, arithmetic and copies ran while one was open for 2% of the time, Pallas kernels for 31%

profile of v4, /device:TPU:18, one launch (start us, length us, event | category | flops | bytes accessed | tf_op | source)
XLA Modules:
  0.0 158.0 jit_solution(13280261286347370420)
XLA Ops:
  0.7 0.6 pad_add_fusion.scalars
  1.3 29.9 %first_planes.1 = (bf16[896,1536]{1,0:T(8,128)(2,1)}, bf16[1536,1536]{1,0:T(8,128)(2,1)}, bf16[896,1536]{1,0:T(8,128)(2,1)}) custom-call(s32[2]{0:T(128)} %pad_add_fusion.scalars), custom_call_target="tpu_custom_call" | custom-call | flops 24999999488 | bytes 8000000 | tf_op jit(solution)/shard_map/first_planes/pallas_call | solution.py:328
  31.1 3.8 %all-to-all-start = ((bf16[8,112,1536]{2,1,0:T(8,128)(2,1)}), bf16[8,112,1536]{2,1,0:T(8,128)(2,1)S(1)}, u32[]{:S(2)}, u32[]{:S(2)}) async-start(bf16[8,112,1536]{2,1,0:T(8,128)(2,1)} %bitcast.4), calls=%async_computation | async-start | bytes 5505024 | tf_op jit(solution)/shard_map/all_to_all | solution.py:694
  35.0 20.5 %more_planes.3 = (bf16[112,1536]{1,0:T(8,128)(2,1)}, bf16[112,1536]{1,0:T(8,128)(2,1)}, bf16[112,1536]{1,0:T(8,128)(2,1)}, bf16[112,1536]{1,0:T(8,128)(2,1)}) custom-call(s32[2]{0:T(128)} %pad_add_fusion.scalars, bf16[1536,1536]{1,0:T(8,128)(2,1)} %get-tuple-element.17.basis_in, bf16[896,1536]{1,0:T(8,128)(2,1)} %get-tuple-element.18.folded_in), custom_call_target="tpu_custom_call" | custom-call | flops 20000000000 | bytes 8000000 | tf_op jit(solution)/shard_map/more_planes/pallas_call | solution.py:388
  55.5 0.6 collective-permute-start.5
  56.1 1.7 %collective-permute-start.6 = (bf16[112,1536]{1,0:T(8,128)(2,1)}, bf16[112,1536]{1,0:T(8,128)(2,1)S(1)}, u32[]{:S(2)}, u32[]{:S(2)}) collective-permute-start(bf16[112,1536]{1,0:T(8,128)(2,1)} %get-tuple-element.25), channel_id=1, source_target_pairs={{0,2},{1,5},{2,0},{3,7},{4,6},{5,1},{6,4},{7,3},{8,10},{9,13},{10,... | collective-permute-start | bytes 1032200 | tf_op jit(solution)/shard_map/ppermute | solution.py:705
  57.8 1.2 collective-permute-start.7
  58.9 1.9 %fusion.1 = (bf16[16,3,1536]{2,1,0:T(4,128)(2,1)S(1)}, bf16[16,3,1536]{2,1,0:T(4,128)(2,1)}) fusion(bf16[16,96,1536]{2,1,0:T(8,128)(2,1)} %f_ref.1), kind=kLoop, calls=%fused_computation.9 | loop fusion | bytes 589824 | tf_op jit(solution)/shard_map/slice | solution.py:716
  60.9 2.3 %collective-permute-start = (bf16[16,3,1536]{2,1,0:T(4,128)(2,1)}, bf16[16,3,1536]{2,1,0:T(4,128)(2,1)}, u32[]{:S(2)}, u32[]{:S(2)}) collective-permute-start(bf16[16,3,1536]{2,1,0:T(4,128)(2,1)} %get-tuple-element.28), channel_id=1, source_target_pairs={{0,1},{1,2},{2,3},{3,4},{4,5},{5,6},{6,7},{7,8},{8,9},{9,10},{10,1... | collective-permute-start | bytes 442376 | tf_op jit(solution)/shard_map/ppermute | solution.py:715
  63.2 4.3 %collective-permute-start.1 = (bf16[16,3,1536]{2,1,0:T(4,128)(2,1)S(1)}, bf16[16,3,1536]{2,1,0:T(4,128)(2,1)}, u32[]{:S(2)}, u32[]{:S(2)}) collective-permute-start(bf16[16,3,1536]{2,1,0:T(4,128)(2,1)S(1)} %get-tuple-element.27), channel_id=1, source_target_pairs={{1,0},{2,1},{3,2},{4,3},{5,4},{6,5},{7,6},{8,7},{9,8},{10,9},{11,1... | collective-permute-start | bytes 442376 | tf_op jit(solution)/shard_map/ppermute | solution.py:716
  67.5 20.5 %more_planes.2 = (bf16[112,1536]{1,0:T(8,128)(2,1)}, bf16[112,1536]{1,0:T(8,128)(2,1)}, bf16[112,1536]{1,0:T(8,128)(2,1)}, bf16[112,1536]{1,0:T(8,128)(2,1)}) custom-call(s32[2]{0:T(128)} %pad_add_fusion.scalars, bf16[1536,1536]{1,0:T(8,128)(2,1)} %get-tuple-element.17.basis_in, bf16[896,1536]{1,0:T(8,128)(2,1)} %get-tuple-element.18.folded_in), custom_call_target="tpu_custom_call" | custom-call | flops 20000000000 | bytes 8000000 | tf_op jit(solution)/shard_map/more_planes/pallas_call | solution.py:388
  88.1 0.1 collective-permute-start.2
  88.1 0.0 collective-permute-done.1.high_ref
  88.1 0.6 collective-permute-start.3
  88.8 0.0 collective-permute-done.5.refs_5_
  88.8 0.1 collective-permute-start.4
  88.9 0.6 compare_select_fusion.slot_modes
  89.5 8.2 %fold.1.forcing = bf16[16,112,1536]{2,1,0:T(8,128)(2,1)} custom-call(bf16[16,96,1536]{2,1,0:T(8,128)(2,1)} %f_ref.1, bf16[16,3,1536]{2,1,0:T(4,128)(2,1)} %collective-permute-done.low_ref, bf16[16,3,1536]{2,1,0:T(4,128)(2,1)} %collective-permute-done.1.high_ref), custom_call_target="tpu_custom_call" | custom-call | flops 1300000000 | bytes 10000000 | tf_op jit(solution)/shard_map/fold/pallas_call | solution.py:435
  97.7 0.0 collective-permute-done.7.refs_7_
  97.8 0.0 collective-permute-done.2.refs_1_
  97.8 0.8 copy-done.3
  98.6 0.4 collective-permute-done.4.refs_3_
  98.9 1.5 copy-done
  100.5 57.4 %solve.1 = bf16[16,96,1536]{2,1,0:T(8,128)(2,1)} custom-call(s32[2]{0:T(128)} %pad_add_fusion.scalars, s32[1,256]{1,0:T(1,128)} %compare_select_fusion.slot_modes, bf16[16,112,1536]{2,1,0:T(8,128)(2,1)} %fold.1.forcing, bf16[8,112,1536]{2,1,0:T(8,128)(2,1)} %copy-done, bf16[112,1536]{1,0:T(8,128)(2,1)} %get-tuple-element.19.refs_0_, ...), custom_call_target="tpu_custom_call" | custom-call | tf_op jit(solution)/shard_map/solve/pallas_call | solution.py:662
  (10 shorter events, 0.0 us)
Async XLA Ops:
  31.1 67.8 %all-to-all-start = ((bf16[8,112,1536]{2,1,0:T(8,128)(2,1)}), bf16[8,112,1536]{2,1,0:T(8,128)(2,1)S(1)}, u32[]{:S(2)}, u32[]{:S(2)}) async-start(bf16[8,112,1536]{2,1,0:T(8,128)(2,1)} %bitcast.4), calls=%async_computation | async-start | bytes 5505024 | tf_op jit(solution)/shard_map/all_to_all | solution.py:694
  55.5 33.3 %collective-permute-start.5 = (bf16[112,1536]{1,0:T(8,128)(2,1)}, bf16[112,1536]{1,0:T(8,128)(2,1)S(1)}, u32[]{:S(2)}, u32[]{:S(2)}) collective-permute-start(bf16[112,1536]{1,0:T(8,128)(2,1)} %get-tuple-element.24), channel_id=1, source_target_pairs={{0,1},{1,0},{2,3},{3,2},{4,5},{5,4},{6,7},{7,6},{8,9},{9,8},{10,11... | collective-permute-start | bytes 1032200 | tf_op jit(solution)/shard_map/ppermute | solution.py:705
  56.1 41.6 %collective-permute-start.6 = (bf16[112,1536]{1,0:T(8,128)(2,1)}, bf16[112,1536]{1,0:T(8,128)(2,1)S(1)}, u32[]{:S(2)}, u32[]{:S(2)}) collective-permute-start(bf16[112,1536]{1,0:T(8,128)(2,1)} %get-tuple-element.25), channel_id=1, source_target_pairs={{0,2},{1,5},{2,0},{3,7},{4,6},{5,1},{6,4},{7,3},{8,10},{9,13},{10,... | collective-permute-start | bytes 1032200 | tf_op jit(solution)/shard_map/ppermute | solution.py:705
  57.8 40.0 %collective-permute-start.7 = (bf16[112,1536]{1,0:T(8,128)(2,1)}, bf16[112,1536]{1,0:T(8,128)(2,1)S(1)}, u32[]{:S(2)}, u32[]{:S(2)}) collective-permute-start(bf16[112,1536]{1,0:T(8,128)(2,1)} %get-tuple-element.26), channel_id=1, source_target_pairs={{0,3},{1,4},{2,1},{3,6},{4,7},{5,0},{6,5},{7,2},{8,11},{9,12},{10,... | collective-permute-start | bytes 1032200 | tf_op jit(solution)/shard_map/ppermute | solution.py:705
  60.9 27.2 %collective-permute-start = (bf16[16,3,1536]{2,1,0:T(4,128)(2,1)}, bf16[16,3,1536]{2,1,0:T(4,128)(2,1)}, u32[]{:S(2)}, u32[]{:S(2)}) collective-permute-start(bf16[16,3,1536]{2,1,0:T(4,128)(2,1)} %get-tuple-element.28), channel_id=1, source_target_pairs={{0,1},{1,2},{2,3},{3,4},{4,5},{5,6},{6,7},{7,8},{8,9},{9,10},{10,1... | collective-permute-start | bytes 442376 | tf_op jit(solution)/shard_map/ppermute | solution.py:715
  63.2 24.9 %collective-permute-start.1 = (bf16[16,3,1536]{2,1,0:T(4,128)(2,1)S(1)}, bf16[16,3,1536]{2,1,0:T(4,128)(2,1)}, u32[]{:S(2)}, u32[]{:S(2)}) collective-permute-start(bf16[16,3,1536]{2,1,0:T(4,128)(2,1)S(1)} %get-tuple-element.27), channel_id=1, source_target_pairs={{1,0},{2,1},{3,2},{4,3},{5,4},{6,5},{7,6},{8,7},{9,8},{10,9},{11,1... | collective-permute-start | bytes 442376 | tf_op jit(solution)/shard_map/ppermute | solution.py:716
  88.1 9.7 %collective-permute-start.2 = (bf16[112,1536]{1,0:T(8,128)(2,1)}, bf16[112,1536]{1,0:T(8,128)(2,1)}, u32[]{:S(2)}, u32[]{:S(2)}) collective-permute-start(bf16[112,1536]{1,0:T(8,128)(2,1)} %get-tuple-element.20), channel_id=1, source_target_pairs={{0,1},{1,0},{2,3},{3,2},{4,5},{5,4},{6,7},{7,6},{8,9},{9,8},{10,11... | collective-permute-start | bytes 1032200 | tf_op jit(solution)/shard_map/ppermute | solution.py:705
  88.1 9.6 %collective-permute-start.3 = (bf16[112,1536]{1,0:T(8,128)(2,1)}, bf16[112,1536]{1,0:T(8,128)(2,1)}, u32[]{:S(2)}, u32[]{:S(2)}) collective-permute-start(bf16[112,1536]{1,0:T(8,128)(2,1)} %get-tuple-element.21), channel_id=1, source_target_pairs={{0,4},{1,3},{2,6},{3,1},{4,0},{5,7},{6,2},{7,5},{8,12},{9,11},{10,... | collective-permute-start | bytes 1032200 | tf_op jit(solution)/shard_map/ppermute | solution.py:705
  88.8 8.9 %copy-start.1 = (bf16[112,1536]{1,0:T(8,128)(2,1)}, bf16[112,1536]{1,0:T(8,128)(2,1)S(1)}, u32[]{:S(2)}) copy-start(bf16[112,1536]{1,0:T(8,128)(2,1)S(1)} %collective-permute-done.5.refs_5_) | copy-start | bytes 1032196
  88.8 10.1 %collective-permute-start.4 = (bf16[112,1536]{1,0:T(8,128)(2,1)}, bf16[112,1536]{1,0:T(8,128)(2,1)}, u32[]{:S(2)}, u32[]{:S(2)}) collective-permute-start(bf16[112,1536]{1,0:T(8,128)(2,1)} %get-tuple-element.22), channel_id=1, source_target_pairs={{0,5},{1,2},{2,7},{3,0},{4,1},{5,6},{6,3},{7,4},{8,13},{9,10},{10,... | collective-permute-start | bytes 1032200 | tf_op jit(solution)/shard_map/ppermute | solution.py:705
  97.7 1.2 copy-start.2
  97.7 0.8 copy-start.3
  98.9 1.5 copy-start
